TPU v7x, 512 devices: a whole 4x8x8 slice. The times are simulated.
512 devices in a mesh: seq: 256 (over z, y, x), head: 2 (over core).
Axes of the slice: x: 4, y: 8, z: 8, core: 2. Of those that a mesh axis runs over, the one named last changes fastest.
Arguments:
- tokens: bfloat16 [65536, 1024], P(('seq', 'head')), may hold values from -30 to 30
- ln1_gain: float32 [1024], replicated, may hold values from 0.5 to 1.5
- ln1_bias: float32 [1024], replicated, may hold values from -3 to 3
- w_qkv: bfloat16 [1024, 3, 1024], P(None, None, 'head'), may hold values from -1 to 1
- w_out: bfloat16 [1024, 1024], P('head'), may hold values from -0.1875 to 0.1875
- ln2_gain: float32 [1024], replicated, may hold values from 0.5 to 1.5
- ln2_bias: float32 [1024], replicated, may hold values from -3 to 3
- w_up: bfloat16 [1024, 4096], P(None, 'head'), may hold values from -0.1875 to 0.1875
- w_down: bfloat16 [4096, 1024], P('head'), may hold values from -0.09375 to 0.09375
- block_mask: int32 [256, 256], replicated, may hold values from 0 to 1, as said below
Outputs:
- layer_out: bfloat16 [65536, 1024], P(('seq', 'head'))
Inputs may be any that keep to these rules, and one draw needn't show every extreme that they name: `block_mask`: the diagonal is 1; every 1 lies within 4 blocks of the diagonal; each row holds 2 to 8 ones, and some row holds exactly 8.
All inputs are finite; a program needn't handle non-finite values.
Results may differ from a plain program's by a relative error of at most 0.0095.
Values may be sent and summed in bfloat16 or wider, within the bound.
No kernel may reach another device: no remote copies, remote signals or barrier semaphores. Data moves between devices by JAX's collectives and lax.ppermute only.
A program may use at most 64 MiB of HBM per device.

v0:
```python
import jax
import jax.numpy as jnp
from jax import lax
from jax.sharding import PartitionSpec as P

HDIM = 64
REACH = 4


norm_eps = 1e-06


def passed_along(array, axis, by):
    size = lax.axis_size(axis)
    pairs = [(i, i + by) for i in range(size) if 0 <= i + by < size]
    return lax.ppermute(array, axis, pairs)


def layer_norm(inputs, gain, shift):
    inputs = inputs.astype(jnp.float32)
    center = inputs - jnp.mean(inputs, axis=-1, keepdims=True)
    spread = jnp.mean(center * center, axis=-1, keepdims=True)
    return center * lax.rsqrt(spread + norm_eps) * gain + shift


def attend(states, query_heads, key_rows, value_rows):
    running_max, running_sum, weighted = states
    query_count = query_heads.shape[0]
    heads_here = query_heads.shape[1]
    key_heads = key_rows.reshape(key_rows.shape[0], heads_here, HDIM)
    value_heads = value_rows.reshape(value_rows.shape[0], heads_here, HDIM)
    scores = jnp.einsum(
        "qhd,khd->hqk", query_heads, key_heads, preferred_element_type=jnp.float32
    ) * HDIM ** (-0.5)
    new_max = jnp.maximum(running_max, jnp.max(scores, axis=2))
    decay = jnp.exp(running_max - new_max)
    weights = jnp.exp(scores - new_max[:, :, None])
    running_sum = running_sum * decay + jnp.sum(weights, axis=2)
    mixture = jnp.einsum(
        "hqk,khd->qhd",
        weights.astype(jnp.bfloat16),
        value_heads,
        preferred_element_type=jnp.float32,
    )
    weighted = weighted.reshape(query_count, heads_here, HDIM) * decay.T[:, :, None] + mixture
    return (new_max, running_sum, weighted.reshape(query_count, heads_here * HDIM))


def shards(tokens, ln1_gain, ln1_bias, w_qkv, w_out, ln2_gain, ln2_bias, w_up, w_down, block_mask):
    tok_rows, width = tokens.shape
    groups = lax.axis_size("head")
    block_rows = tok_rows * groups
    head_cols = w_qkv.shape[2]
    heads_here = head_cols // HDIM
    normed_one = layer_norm(tokens, ln1_gain, ln1_bias).astype(jnp.bfloat16)
    flat_qkv = w_qkv.reshape(width, 3 * head_cols)
    packed = jnp.dot(
        lax.all_gather(normed_one, "head", axis=0, tiled=True),
        flat_qkv,
        preferred_element_type=jnp.float32,
    ).astype(jnp.bfloat16)
    query_heads = packed[:, :head_cols].reshape(block_rows, heads_here, HDIM)
    key_rows = packed[:, head_cols : 2 * head_cols]
    value_rows = packed[:, 2 * head_cols :]
    block_count = lax.axis_size("seq")
    here = lax.axis_index("seq")
    mask_row = lax.dynamic_index_in_dim(block_mask, here, 0, keepdims=False)
    initial = (
        jnp.full((heads_here, block_rows), -1e30, jnp.float32),
        jnp.zeros((heads_here, block_rows), jnp.float32),
        jnp.zeros((block_rows, head_cols), jnp.float32),
    )
    final = attend(initial, query_heads, key_rows, value_rows)
    for offset in list(range(-REACH, 0)) + list(range(1, REACH + 1)):
        key_near, value_near = passed_along((key_rows, value_rows), "seq", offset)
        source = here - offset
        inside = (source >= 0) & (source < block_count)
        listed = jnp.where(inside, mask_row[jnp.clip(source, 0, block_count - 1)], 0)
        final = lax.cond(
            listed > 0,
            lambda inner: attend(inner, query_heads, key_near, value_near),
            lambda inner: inner,
            final,
        )
    running_max, running_sum, weighted = final
    attended = (
        (weighted.reshape(block_rows, heads_here, HDIM) / running_sum.T[:, :, None])
        .reshape(block_rows, head_cols)
        .astype(jnp.bfloat16)
    )
    picked = attended
    projected = lax.psum_scatter(
        jnp.dot(picked, w_out, preferred_element_type=jnp.float32).astype(jnp.bfloat16),
        "head",
        scatter_dimension=0,
        tiled=True,
    ).astype(jnp.float32)
    resid = (tokens.astype(jnp.float32) + projected).astype(jnp.bfloat16)
    normed_two = layer_norm(resid, ln2_gain, ln2_bias).astype(jnp.bfloat16)
    hidden = jax.nn.gelu(
        jnp.dot(
            lax.all_gather(normed_two, "head", axis=0, tiled=True),
            w_up,
            preferred_element_type=jnp.float32,
        ),
        approximate=False,
    ).astype(jnp.bfloat16)
    picked = hidden
    mlp_part = lax.psum_scatter(
        jnp.dot(picked, w_down, preferred_element_type=jnp.float32).astype(jnp.bfloat16),
        "head",
        scatter_dimension=0,
        tiled=True,
    ).astype(jnp.float32)
    return (resid.astype(jnp.float32) + mlp_part).astype(jnp.bfloat16)


def solution(mesh):
    in_specs = (
        P(("seq", "head"), None),
        P(),
        P(),
        P(None, None, "head"),
        P("head", None),
        P(),
        P(),
        P(None, "head"),
        P("head", None),
        P(),
    )
    out_specs = P(("seq", "head"), None)
    return jax.shard_map(shards, mesh=mesh, in_specs=in_specs, out_specs=out_specs, check_vma=False)
```

profile of v0, /device:TPU:1, one launch (start us, length us, event | category | flops | bytes accessed | tf_op | source)
XLA Modules:
  0.0 198.6 jit_solution(16953157082429559721)
XLA Ops:
  6.5 1.2 convert_reduce_fusion.1
  7.7 1.2 fusion.119
  8.9 1.2 fusion.122
  10.1 8.6 %all_gather.6 = bf16[256,1024]{1,0:T(8,128)(2,1)S(1)} all-gather(bf16[128,1024]{1,0:T(8,128)(2,1)S(1)} %fusion.122), channel_id=1, replica_groups=mesh['seq'=256,'head'=2] {'head'}, dimensions={0}, use_global_device_ids=true | all-gather | bytes 786432 | tf_op jit(solution)/shard_map/all_gather | solution.py:58
  18.7 4.6 %copy.55 = bf16[1024,3,512]{0,2,1:T(8,128)(2,1)} copy(bf16[1024,3,512]{2,0,1:T(8,128)(2,1)} %param.29) | data formatting | bytes 6291456 | tf_op args[3]
  23.4 2.9 %convolution_convert_fusion = bf16[256,1536]{1,0:T(8,128)(2,1)S(1)} fusion(bf16[256,1024]{1,0:T(8,128)(2,1)S(1)} %all_gather.6, bf16[1024,1536]{0,1:T(8,128)(2,1)} %bitcast.162), kind=kOutput, calls=%fused_computation.97 | convolution fusion | flops 805699584 | bytes 4456448 | tf_op jit(solution)/shard_map/dot_general | solution.py:57
  26.3 0.1 fusion.160
  26.4 1.3 collective-permute-start
  27.7 1.3 collective-permute-start.2
  29.0 1.3 collective-permute-start.1
  30.3 1.3 collective-permute-start.3
  31.6 1.3 collective-permute-start.4
  32.9 0.1 copy.57
  33.0 0.1 copy.56
  33.2 2.6 %collective-permute-done = bf16[256,512]{1,0:T(8,128)(2,1)S(1)} collective-permute-done((bf16[256,512]{1,0:T(8,128)(2,1)S(1)}, bf16[256,512]{1,0:T(8,128)(2,1)S(1)}, u32[]{:S(2)}, u32[]{:S(2)}) %collective-permute-start) | collective-permute-done | bytes 262176 | tf_op jit(solution)/shard_map/ppermute | solution.py:16
  35.8 1.3 collective-permute-start.5
  37.1 0.5 multiply_reduce_fusion.8
  37.6 9.5 %collective-permute-done.1 = bf16[256,512]{1,0:T(8,128)(2,1)S(1)} collective-permute-done((bf16[256,512]{1,0:T(8,128)(2,1)S(1)}, bf16[256,512]{1,0:T(8,128)(2,1)S(1)}, u32[]{:S(2)}, u32[]{:S(2)}) %collective-permute-start.1) | collective-permute-done | bytes 262176 | tf_op jit(solution)/shard_map/ppermute | solution.py:16
  47.1 1.3 collective-permute-start.6
  48.4 0.0 collective-permute-done.2
  48.4 1.3 collective-permute-start.7
  49.7 0.0 collective-permute-done.3
  49.7 6.1 %collective-permute-start.8 = (bf16[256,512]{1,0:T(8,128)(2,1)S(1)}, bf16[256,512]{1,0:T(8,128)(2,1)S(1)}, u32[]{:S(2)}, u32[]{:S(2)}) collective-permute-start(bf16[256,512]{1,0:T(8,128)(2,1)S(1)} %get-tuple-element.372), channel_id=1, source_target_pairs={{0,2},{2,4},{4,6},{6,8},{8,10},{10,12},{12,14},{14,16},{16,18},{18... | collective-permute-start | bytes 786440 | tf_op jit(solution)/shard_map/ppermute | solution.py:16
  55.8 0.0 collective-permute-done.4
  55.8 1.9 collective-permute-start.9
  57.8 0.0 collective-permute-done.5
  57.8 10.8 %collective-permute-start.10 = (bf16[256,512]{1,0:T(8,128)(2,1)S(1)}, bf16[256,512]{1,0:T(8,128)(2,1)S(1)}, u32[]{:S(2)}, u32[]{:S(2)}) collective-permute-start(bf16[256,512]{1,0:T(8,128)(2,1)S(1)} %get-tuple-element.372), channel_id=1, source_target_pairs={{0,4},{2,6},{4,8},{6,10},{8,12},{10,14},{12,16},{14,18},{16,20},{1... | collective-permute-start | bytes 786440 | tf_op jit(solution)/shard_map/ppermute | solution.py:16
  68.6 0.4 fusion.75
  69.0 0.1 copy.58
  69.2 1.7 fusion.161
  75.8 0.0 collective-permute-done.6
  75.8 2.6 %collective-permute-start.11 = (bf16[256,512]{1,0:T(8,128)(2,1)S(1)}, bf16[256,512]{1,0:T(8,128)(2,1)}, u32[]{:S(2)}, u32[]{:S(2)}) collective-permute-start(bf16[256,512]{1,0:T(8,128)(2,1)S(1)} %get-tuple-element.371), channel_id=1, source_target_pairs={{0,4},{2,6},{4,8},{6,10},{8,12},{10,14},{12,16},{14,18},{16,20},{1... | collective-permute-start | bytes 786440 | tf_op jit(solution)/shard_map/ppermute | solution.py:16
  78.4 0.0 collective-permute-done.7
  78.4 5.0 %collective-permute-start.12 = (bf16[256,512]{1,0:T(8,128)(2,1)S(1)}, bf16[256,512]{1,0:T(8,128)(2,1)}, u32[]{:S(2)}, u32[]{:S(2)}) collective-permute-start(bf16[256,512]{1,0:T(8,128)(2,1)S(1)} %get-tuple-element.372), channel_id=1, source_target_pairs={{0,6},{2,8},{4,10},{6,12},{8,14},{10,16},{12,18},{14,20},{16,22},{... | collective-permute-start | bytes 786440 | tf_op jit(solution)/shard_map/ppermute | solution.py:16
  83.5 0.0 collective-permute-done.8
  83.5 2.0 %collective-permute-start.13 = (bf16[256,512]{1,0:T(8,128)(2,1)S(1)}, bf16[256,512]{1,0:T(8,128)(2,1)}, u32[]{:S(2)}, u32[]{:S(2)}) collective-permute-start(bf16[256,512]{1,0:T(8,128)(2,1)S(1)} %get-tuple-element.371), channel_id=1, source_target_pairs={{0,6},{2,8},{4,10},{6,12},{8,14},{10,16},{12,18},{14,20},{16,22},{... | collective-permute-start | bytes 786440 | tf_op jit(solution)/shard_map/ppermute | solution.py:16
  85.4 2.0 %collective-permute-start.14 = (bf16[256,512]{1,0:T(8,128)(2,1)S(1)}, bf16[256,512]{1,0:T(8,128)(2,1)}, u32[]{:S(2)}, u32[]{:S(2)}) collective-permute-start(bf16[256,512]{1,0:T(8,128)(2,1)S(1)} %get-tuple-element.372), channel_id=1, source_target_pairs={{0,8},{2,10},{4,12},{6,14},{8,16},{10,18},{12,20},{14,22},{16,24},... | collective-permute-start | bytes 786440 | tf_op jit(solution)/shard_map/ppermute | solution.py:16
  87.4 2.4 %collective-permute-start.15 = (bf16[256,512]{1,0:T(8,128)(2,1)S(1)}, bf16[256,512]{1,0:T(8,128)(2,1)}, u32[]{:S(2)}, u32[]{:S(2)}) collective-permute-start(bf16[256,512]{1,0:T(8,128)(2,1)S(1)} %get-tuple-element.371), channel_id=1, source_target_pairs={{0,8},{2,10},{4,12},{6,14},{8,16},{10,18},{12,20},{14,22},{16,24},... | collective-permute-start | bytes 786440 | tf_op jit(solution)/shard_map/ppermute | solution.py:16
  89.8 2.1 %fusion.76 = f32[256,8,64]{0,2,1:T(8,128)S(1)} fusion(bf16[256,8,64]{0,2,1:T(8,128)(2,1)S(1)} %bitcast.172, f32[8,256,256]{1,2,0:T(8,128)} %copy-done.1, f32[8,256]{1,0:T(8,128)S(1)} %broadcast_maximum_fusion, f32[256,8]{0,1:T(8,128)S(1)} %get-tuple-element.382), kind=kOutput, calls=%fused_computation.123 | convolution fusion | flops 68812800 | bytes 2899968 | tf_op jit(solution)/shard_map/hqk,khd->qhd/dot_general | solution.py:39
  92.0 6.6 %conditional.10 = ((f32[8,256]{1,0:T(8,128)S(1)}, f32[8,256]{1,0:T(8,128)S(1)}, f32[256,512]{0,1:T(8,128)S(1)})) conditional(s32[]{:T(128)} %convert_element_type.98, (f32[8,256]{1,0:T(8,128)S(1)}, f32[8,256]{1,0:T(8,128)S(1)}, f32[256,512]{0,1:T(8,128)S(1)}) %get-tuple-element.439, (bf16[256,512]{1,0:T(8,128)(2,1)}, ...), branch_computations={%region_12.13_spmd, %region_13.16_spmd} | conditional | flops 138680320 | bytes 17694780 | solution.py:79
  92.0 1.1 copy.64
  93.1 0.5 multiply_reduce_fusion.2
  93.6 1.3 copy-done.4
  94.9 0.4 fusion.17
  95.3 1.1 copy.65
  96.4 2.1 %fusion.18 = f32[256,8,64]{0,2,1:T(8,128)S(1)} fusion(bf16[256,8,64]{0,2,1:T(8,128)(2,1)S(1)} %bitcast.175, f32[8,256,256]{1,2,0:T(8,128)} %copy-done.4, f32[8,256]{1,0:T(8,128)S(1)} %get-tuple-element.401, f32[256,8,64]{0,2,1:T(8,128)S(1)} %bitcast.141, f32[256,8]{0,1:T(8,128)S(1)} %get-tuple-element.341), kind=kOutput, calls=%fused_computation.29 | convolution fusion | flops 68943872 | bytes 3424256 | tf_op jit(solution)/shard_map/cond/branch_1_fun/hqk,khd->qhd/dot_general | solution.py:39
  98.6 0.2 conditional.12
  98.8 0.0 collective-permute-done.12
  98.8 0.0 collective-permute-done.14
  98.9 0.0 copy-start.10
  98.9 0.0 copy-start.17
  98.9 0.0 copy-start.18
  99.0 1.3 convolution_convert_fusion.1
  100.2 0.0 reduce-scatter.3.cloned.1.call-update
  100.3 0.0 reduce-scatter.5.cloned.1.call-start
  100.3 57.4 %reduce-scatter.3.cloned.1.call-done = bf16[128,1024]{1,0:T(8,128)(2,1)} async-done(((bf16[256,1024]{1,0:T(8,128)(2,1)}), bf16[128,1024]{1,0:T(8,128)(2,1)}) %reduce-scatter.3.cloned.1.call-update) | async-done | bytes 262160 | tf_op jit(solution)/shard_map/reduce_scatter | solution.py:92
  157.7 1.1 convert_reduce_fusion
  158.8 0.2 fusion.115
  159.0 0.2 fusion.118
  159.3 2.4 %all_gather.7 = bf16[256,1024]{1,0:T(8,128)(2,1)S(1)} all-gather(bf16[128,1024]{1,0:T(8,128)(2,1)S(1)} %fusion.118), channel_id=1, replica_groups=mesh['seq'=256,'head'=2] {'head'}, dimensions={0}, use_global_device_ids=true | all-gather | bytes 786432 | tf_op jit(solution)/shard_map/all_gather | solution.py:102
  161.7 10.8 %convolution_convert_fusion.2 = bf16[256,1024]{1,0:T(8,128)(2,1)} fusion(bf16[2048,1024]{1,0:T(8,128)(2,1)} %param.34, bf16[256,1024]{1,0:T(8,128)(2,1)S(1)} %all_gather.7, bf16[1024,2048]{1,0:T(8,128)(2,1)} %param.33), kind=kOutput, calls=%fused_computation.121 | convolution fusion | flops 2181824512 | bytes 9437184 | tf_op jit(solution)/shard_map/dot_general | solution.py:110
  172.5 0.0 reduce-scatter.5.cloned.1.call-update
  172.5 17.5 %reduce-scatter.5.cloned.1.call-done = bf16[128,1024]{1,0:T(8,128)(2,1)} async-done(((bf16[256,1024]{1,0:T(8,128)(2,1)}), bf16[128,1024]{1,0:T(8,128)(2,1)}) %reduce-scatter.5.cloned.1.call-update) | async-done | bytes 262160 | tf_op jit(solution)/shard_map/reduce_scatter | solution.py:109
  190.0 1.7 fusion.124
  (42 shorter events, 0.2 us)
Async XLA Ops:
  6.5 92.4 %copy-start = (bf16[512,1024]{1,0:T(8,128)(2,1)S(1)}, bf16[512,1024]{1,0:T(8,128)(2,1)}, u32[]{:S(2)}) copy-start(bf16[512,1024]{1,0:T(8,128)(2,1)} %param.30) | copy-start | bytes 3145732
  6.5 151.1 %reduce-scatter.3.cloned.1.call-start = ((), (), s32[]{:S(2)}) async-start(), calls=%async_computation.2 | async-start | bytes 786432 | tf_op jit(solution)/shard_map/reduce_scatter | solution.py:92
  26.4 9.4 %collective-permute-start = (bf16[256,512]{1,0:T(8,128)(2,1)S(1)}, bf16[256,512]{1,0:T(8,128)(2,1)S(1)}, u32[]{:S(2)}, u32[]{:S(2)}) collective-permute-start(bf16[256,512]{1,0:T(8,128)(2,1)S(1)} %get-tuple-element.372), channel_id=1, source_target_pairs={{8,0},{10,2},{12,4},{14,6},{16,8},{18,10},{20,12},{22,14},{24,16},... | collective-permute-start | bytes 786440 | tf_op jit(solution)/shard_map/ppermute | solution.py:16
  27.7 20.7 %collective-permute-start.2 = (bf16[256,512]{1,0:T(8,128)(2,1)S(1)}, bf16[256,512]{1,0:T(8,128)(2,1)S(1)}, u32[]{:S(2)}, u32[]{:S(2)}) collective-permute-start(bf16[256,512]{1,0:T(8,128)(2,1)S(1)} %get-tuple-element.372), channel_id=1, source_target_pairs={{6,0},{8,2},{10,4},{12,6},{14,8},{16,10},{18,12},{20,14},{22,16},{... | collective-permute-start | bytes 786440 | tf_op jit(solution)/shard_map/ppermute | solution.py:16
  29.0 18.1 %collective-permute-start.1 = (bf16[256,512]{1,0:T(8,128)(2,1)S(1)}, bf16[256,512]{1,0:T(8,128)(2,1)S(1)}, u32[]{:S(2)}, u32[]{:S(2)}) collective-permute-start(bf16[256,512]{1,0:T(8,128)(2,1)S(1)} %get-tuple-element.371), channel_id=1, source_target_pairs={{8,0},{10,2},{12,4},{14,6},{16,8},{18,10},{20,12},{22,14},{24,16},... | collective-permute-start | bytes 786440 | tf_op jit(solution)/shard_map/ppermute | solution.py:16
  30.3 19.5 %collective-permute-start.3 = (bf16[256,512]{1,0:T(8,128)(2,1)S(1)}, bf16[256,512]{1,0:T(8,128)(2,1)}, u32[]{:S(2)}, u32[]{:S(2)}) collective-permute-start(bf16[256,512]{1,0:T(8,128)(2,1)S(1)} %get-tuple-element.371), channel_id=1, source_target_pairs={{6,0},{8,2},{10,4},{12,6},{14,8},{16,10},{18,12},{20,14},{22,16},{... | collective-permute-start | bytes 786440 | tf_op jit(solution)/shard_map/ppermute | solution.py:16
  31.6 24.2 %collective-permute-start.4 = (bf16[256,512]{1,0:T(8,128)(2,1)S(1)}, bf16[256,512]{1,0:T(8,128)(2,1)S(1)}, u32[]{:S(2)}, u32[]{:S(2)}) collective-permute-start(bf16[256,512]{1,0:T(8,128)(2,1)S(1)} %get-tuple-element.372), channel_id=1, source_target_pairs={{4,0},{6,2},{8,4},{10,6},{12,8},{14,10},{16,12},{18,14},{20,16},{2... | collective-permute-start | bytes 786440 | tf_op jit(solution)/shard_map/ppermute | solution.py:16
  35.8 14.0 %copy-start.15 = (bf16[256,512]{1,0:T(8,128)(2,1)}, bf16[256,512]{1,0:T(8,128)(2,1)S(1)}, u32[]{:S(2)}) copy-start(bf16[256,512]{1,0:T(8,128)(2,1)S(1)} %collective-permute-done) | copy-start | bytes 786436
  35.8 22.0 %collective-permute-start.5 = (bf16[256,512]{1,0:T(8,128)(2,1)S(1)}, bf16[256,512]{1,0:T(8,128)(2,1)}, u32[]{:S(2)}, u32[]{:S(2)}) collective-permute-start(bf16[256,512]{1,0:T(8,128)(2,1)S(1)} %get-tuple-element.371), channel_id=1, source_target_pairs={{4,0},{6,2},{8,4},{10,6},{12,8},{14,10},{16,12},{18,14},{20,16},{2... | collective-permute-start | bytes 786440 | tf_op jit(solution)/shard_map/ppermute | solution.py:16
  37.5 31.1 %copy-start.1 = (f32[8,256,256]{1,2,0:T(8,128)}, f32[8,256,256]{1,2,0:T(8,128)S(1)}, u32[]{:S(2)}) copy-start(f32[8,256,256]{1,2,0:T(8,128)S(1)} %get-tuple-element.385) | copy-start | bytes 6291460
  47.1 2.6 %copy-start.16 = (bf16[256,512]{1,0:T(8,128)(2,1)}, bf16[256,512]{1,0:T(8,128)(2,1)S(1)}, u32[]{:S(2)}) copy-start(bf16[256,512]{1,0:T(8,128)(2,1)S(1)} %collective-permute-done.1) | copy-start | bytes 786436
  47.1 28.7 %collective-permute-start.6 = (bf16[256,512]{1,0:T(8,128)(2,1)S(1)}, bf16[256,512]{1,0:T(8,128)(2,1)S(1)}, u32[]{:S(2)}, u32[]{:S(2)}) collective-permute-start(bf16[256,512]{1,0:T(8,128)(2,1)S(1)} %get-tuple-element.372), channel_id=1, source_target_pairs={{2,0},{4,2},{6,4},{8,6},{10,8},{12,10},{14,12},{16,14},{18,16},{20... | collective-permute-start | bytes 786440 | tf_op jit(solution)/shard_map/ppermute | solution.py:16
  48.4 9.4 %copy-start.14 = (bf16[256,512]{1,0:T(8,128)(2,1)}, bf16[256,512]{1,0:T(8,128)(2,1)S(1)}, u32[]{:S(2)}) copy-start(bf16[256,512]{1,0:T(8,128)(2,1)S(1)} %collective-permute-done.2) | copy-start | bytes 786436
  48.4 30.0 %collective-permute-start.7 = (bf16[256,512]{1,0:T(8,128)(2,1)S(1)}, bf16[256,512]{1,0:T(8,128)(2,1)S(1)}, u32[]{:S(2)}, u32[]{:S(2)}) collective-permute-start(bf16[256,512]{1,0:T(8,128)(2,1)S(1)} %get-tuple-element.371), channel_id=1, source_target_pairs={{2,0},{4,2},{6,4},{8,6},{10,8},{12,10},{14,12},{16,14},{18,16},{20... | collective-permute-start | bytes 786440 | tf_op jit(solution)/shard_map/ppermute | solution.py:16
  49.7 33.7 %collective-permute-start.8 = (bf16[256,512]{1,0:T(8,128)(2,1)S(1)}, bf16[256,512]{1,0:T(8,128)(2,1)S(1)}, u32[]{:S(2)}, u32[]{:S(2)}) collective-permute-start(bf16[256,512]{1,0:T(8,128)(2,1)S(1)} %get-tuple-element.372), channel_id=1, source_target_pairs={{0,2},{2,4},{4,6},{6,8},{8,10},{10,12},{12,14},{14,16},{16,18},{18... | collective-permute-start | bytes 786440 | tf_op jit(solution)/shard_map/ppermute | solution.py:16
  55.8 13.2 %copy-start.13 = (bf16[256,512]{1,0:T(8,128)(2,1)}, bf16[256,512]{1,0:T(8,128)(2,1)S(1)}, u32[]{:S(2)}) copy-start(bf16[256,512]{1,0:T(8,128)(2,1)S(1)} %collective-permute-done.4) | copy-start | bytes 786436
  55.8 29.6 %collective-permute-start.9 = (bf16[256,512]{1,0:T(8,128)(2,1)S(1)}, bf16[256,512]{1,0:T(8,128)(2,1)S(1)}, u32[]{:S(2)}, u32[]{:S(2)}) collective-permute-start(bf16[256,512]{1,0:T(8,128)(2,1)S(1)} %get-tuple-element.371), channel_id=1, source_target_pairs={{0,2},{2,4},{4,6},{6,8},{8,10},{10,12},{12,14},{14,16},{16,18},{18... | collective-permute-start | bytes 786440 | tf_op jit(solution)/shard_map/ppermute | solution.py:16
  57.8 29.7 %collective-permute-start.10 = (bf16[256,512]{1,0:T(8,128)(2,1)S(1)}, bf16[256,512]{1,0:T(8,128)(2,1)S(1)}, u32[]{:S(2)}, u32[]{:S(2)}) collective-permute-start(bf16[256,512]{1,0:T(8,128)(2,1)S(1)} %get-tuple-element.372), channel_id=1, source_target_pairs={{0,4},{2,6},{4,8},{6,10},{8,12},{10,14},{12,16},{14,18},{16,20},{1... | collective-permute-start | bytes 786440 | tf_op jit(solution)/shard_map/ppermute | solution.py:16
  75.8 14.1 %copy-start.11 = (bf16[256,512]{1,0:T(8,128)(2,1)}, bf16[256,512]{1,0:T(8,128)(2,1)S(1)}, u32[]{:S(2)}) copy-start(bf16[256,512]{1,0:T(8,128)(2,1)S(1)} %collective-permute-done.6) | copy-start | bytes 786436
  75.8 23.0 %collective-permute-start.11 = (bf16[256,512]{1,0:T(8,128)(2,1)S(1)}, bf16[256,512]{1,0:T(8,128)(2,1)}, u32[]{:S(2)}, u32[]{:S(2)}) collective-permute-start(bf16[256,512]{1,0:T(8,128)(2,1)S(1)} %get-tuple-element.371), channel_id=1, source_target_pairs={{0,4},{2,6},{4,8},{6,10},{8,12},{10,14},{12,16},{14,18},{16,20},{1... | collective-permute-start | bytes 786440 | tf_op jit(solution)/shard_map/ppermute | solution.py:16
  78.4 11.4 %copy-start.12 = (bf16[256,512]{1,0:T(8,128)(2,1)}, bf16[256,512]{1,0:T(8,128)(2,1)S(1)}, u32[]{:S(2)}) copy-start(bf16[256,512]{1,0:T(8,128)(2,1)S(1)} %collective-permute-done.7) | copy-start | bytes 786436
  78.4 20.3 %collective-permute-start.12 = (bf16[256,512]{1,0:T(8,128)(2,1)S(1)}, bf16[256,512]{1,0:T(8,128)(2,1)}, u32[]{:S(2)}, u32[]{:S(2)}) collective-permute-start(bf16[256,512]{1,0:T(8,128)(2,1)S(1)} %get-tuple-element.372), channel_id=1, source_target_pairs={{0,6},{2,8},{4,10},{6,12},{8,14},{10,16},{12,18},{14,20},{16,22},{... | collective-permute-start | bytes 786440 | tf_op jit(solution)/shard_map/ppermute | solution.py:16
  83.5 15.3 %collective-permute-start.13 = (bf16[256,512]{1,0:T(8,128)(2,1)S(1)}, bf16[256,512]{1,0:T(8,128)(2,1)}, u32[]{:S(2)}, u32[]{:S(2)}) collective-permute-start(bf16[256,512]{1,0:T(8,128)(2,1)S(1)} %get-tuple-element.371), channel_id=1, source_target_pairs={{0,6},{2,8},{4,10},{6,12},{8,14},{10,16},{12,18},{14,20},{16,22},{... | collective-permute-start | bytes 786440 | tf_op jit(solution)/shard_map/ppermute | solution.py:16
  85.4 13.4 %collective-permute-start.14 = (bf16[256,512]{1,0:T(8,128)(2,1)S(1)}, bf16[256,512]{1,0:T(8,128)(2,1)}, u32[]{:S(2)}, u32[]{:S(2)}) collective-permute-start(bf16[256,512]{1,0:T(8,128)(2,1)S(1)} %get-tuple-element.372), channel_id=1, source_target_pairs={{0,8},{2,10},{4,12},{6,14},{8,16},{10,18},{12,20},{14,22},{16,24},... | collective-permute-start | bytes 786440 | tf_op jit(solution)/shard_map/ppermute | solution.py:16
  87.4 11.4 %collective-permute-start.15 = (bf16[256,512]{1,0:T(8,128)(2,1)S(1)}, bf16[256,512]{1,0:T(8,128)(2,1)}, u32[]{:S(2)}, u32[]{:S(2)}) collective-permute-start(bf16[256,512]{1,0:T(8,128)(2,1)S(1)} %get-tuple-element.371), channel_id=1, source_target_pairs={{0,8},{2,10},{4,12},{6,14},{8,16},{10,18},{12,20},{14,22},{16,24},... | collective-permute-start | bytes 786440 | tf_op jit(solution)/shard_map/ppermute | solution.py:16
  93.6 1.3 copy-start.4
  98.9 58.8 %copy-start.10 = (bf16[128,1024]{1,0:T(8,128)(2,1)S(1)}, bf16[128,1024]{1,0:T(8,128)(2,1)}, u32[]{:S(2)}) copy-start(bf16[128,1024]{1,0:T(8,128)(2,1)} %param.26) | copy-start | bytes 786436
  98.9 60.2 %copy-start.17 = (f32[1024]{0:T(1024)S(1)}, f32[1024]{0:T(1024)}, u32[]{:S(2)}) copy-start(f32[1024]{0:T(1024)} %param.32) | copy-start | bytes 12292
  98.9 60.1 %copy-start.18 = (f32[1024]{0:T(1024)S(1)}, f32[1024]{0:T(1024)}, u32[]{:S(2)}) copy-start(f32[1024]{0:T(1024)} %param.31) | copy-start | bytes 12292
  100.3 89.7 %reduce-scatter.5.cloned.1.call-start = ((), (), s32[]{:S(2)}) async-start(), calls=%async_computation.3 | async-start | bytes 786432 | tf_op jit(solution)/shard_map/reduce_scatter | solution.py:109
Sparse Core Ops, SparseCore 0:
  100.4 57.2 reduce-scatter.2
  172.6 17.3 reduce-scatter.4
where the time goes:
time: 200 us; the launch traced here: 199 us
  waiting for transfers between devices  87.1 us (44%)
  starting transfers between devices  43.2 us (22%)
  matrix products  20.2 us (10%)
  between operations  18.8 us (9%)
  blocking collectives  11 us (6%)
  local copies, waits for them, and re-layouts  10.3 us (5%)
  other arithmetic  7.65 us (4%)
    reduce_scatter x1, waiting for transfers between devices, shards(): lax.psum_scatter(jnp.dot(picked, w_out, preferred_element_type=jnp.float3...  57.4 us
    ppermute x16, starting transfers between devices, passed_along(): return lax.ppermute(array, axis, pairs)  43.1 us
    reduce_scatter x1, waiting for transfers between devices, shards(): lax.psum_scatter(jnp.dot(picked, w_down, preferred_element_type=jnp.float...  17.5 us
    ppermute x16, waiting for transfers between devices, passed_along(): return lax.ppermute(array, axis, pairs)  12.2 us
    dot_general x1, matrix products, shards(): jnp.dot(picked, w_down, preferred_element_type=jnp.float32)  10.8 us
    all_gather x1, blocking collectives, shards(): lax.all_gather(normed_one, 'head', axis=0, tiled=True)  8.65 us
    unnamed x23, local copies, waits for them, and re-layouts  4.7 us
    dot_general x2, matrix products, attend(): jnp.einsum('hqk,khd->qhd', weights.astype(jnp.bfloat16), value_heads, pre...  4.21 us
  transfers between devices with their start and end apart: 18, of which 4 were waited for; matrix products, arithmetic and copies ran while one was open for 5% of the time, Pallas kernels for 0%

commit v1 on v0

v1 whole, which is shorter than its diff:
```python
import math

import jax
import jax.numpy as jnp
from jax import lax
from jax.experimental import pallas as pl
from jax.experimental.pallas import tpu as pltpu
from jax.sharding import PartitionSpec as P


HDIM = 64
REACH = 4
LANES = 128
STEP_COLS = 256
EXP_SCALE = HDIM ** (-0.5) * math.log2(math.e)
F32 = jnp.float32
BF16 = jnp.bfloat16

norm_eps = 1e-06


def layer_norm(inputs, gain, shift):
    inputs = inputs.astype(F32)
    center = inputs - jnp.mean(inputs, axis=-1, keepdims=True)
    spread = jnp.mean(center * center, axis=-1, keepdims=True)
    return center * lax.rsqrt(spread + norm_eps) * gain + shift


def dot(left, right):
    return jnp.dot(left, right, preferred_element_type=F32)


def norm_kernel(tokens_ref, gain_ref, bias_ref, out_ref):
    out_ref[...] = layer_norm(tokens_ref[...], gain_ref[...], bias_ref[...]).astype(BF16)


def norm_rows(tokens, gain, bias):
    return pl.pallas_call(
        norm_kernel,
        out_shape=jax.ShapeDtypeStruct(tokens.shape, BF16),
        name="norm_rows",
    )(tokens, gain.reshape(1, -1), bias.reshape(1, -1))


def attend_pair(query_pair, key_pair, value_pair, old_max, old_sum, old_acc):
    rows = query_pair.shape[0]
    first = lax.broadcasted_iota(jnp.int32, (rows, LANES), 1) < HDIM
    zero = jnp.zeros_like(query_pair)
    stacked = jnp.concatenate(
        [jnp.where(first, query_pair, zero), jnp.where(first, zero, query_pair)], axis=0
    )
    scores = (
        lax.dot_general(stacked, key_pair, (((1,), (1,)), ((), ())), preferred_element_type=F32)
        * EXP_SCALE
    )
    new_max = jnp.max(scores, axis=1, keepdims=True)
    if old_max is not None:
        new_max = jnp.maximum(old_max, new_max)
    weights = jnp.exp2(scores - new_max)
    new_sum = jnp.sum(weights, axis=1, keepdims=True)
    mixture = dot(weights.astype(BF16), value_pair)
    mixed = jnp.where(first, mixture[:rows], mixture[rows:])
    if old_max is not None:
        decay = jnp.exp2(old_max - new_max)
        new_sum = new_sum + old_sum * decay
        mixed = mixed + old_acc * jnp.where(first, decay[:rows], decay[rows:])
    return new_max, new_sum, mixed


def attend_step(queries, rows, w_key, w_value, stats_in, acc_in, stats_ref, acc_ref):
    keys = dot(rows, w_key).astype(BF16)
    values = dot(rows, w_value).astype(BF16)
    count = queries.shape[0]
    for pair in range(STEP_COLS // LANES):
        cols = slice(pair * LANES, (pair + 1) * LANES)
        old_max = old_sum = old_acc = None
        if stats_in is not None:
            lane = 4 * pair
            old_max = jnp.concatenate(
                [stats_in[0, :, lane : lane + 1], stats_in[0, :, lane + 1 : lane + 2]], axis=0
            )
            old_sum = jnp.concatenate(
                [stats_in[0, :, lane + 2 : lane + 3], stats_in[0, :, lane + 3 : lane + 4]], axis=0
            )
            old_acc = acc_in[:, cols]
        new_max, new_sum, mixed = attend_pair(
            queries[:, cols], keys[:, cols], values[:, cols], old_max, old_sum, old_acc
        )
        lane = 4 * pair
        stats_ref[0, :, lane : lane + 1] = new_max[:count]
        stats_ref[0, :, lane + 1 : lane + 2] = new_max[count:]
        stats_ref[0, :, lane + 2 : lane + 3] = new_sum[:count]
        stats_ref[0, :, lane + 3 : lane + 4] = new_sum[count:]
        acc_ref[:, cols] = mixed


def own_kernel(
    both_ref, mine_ref, w_own_ref, w_other_ref, query_ref, acc_ref, stats_ref
):
    step = pl.program_id(0)

    def work(weights):
        queries = dot(both_ref[...], weights[0]).astype(BF16)
        query_ref[...] = queries
        attend_step(
            queries, mine_ref[...], weights[1], weights[2], None, None, stats_ref, acc_ref
        )

    half = pl.num_programs(0) // 2

    @pl.when(step < half)
    def _():
        work(w_own_ref)

    @pl.when(step >= half)
    def _():
        work(w_other_ref)


def own_attention(both, mine, w_own, w_other):
    rows, width = both.shape
    steps = width // STEP_COLS
    half = steps // 2
    return pl.pallas_call(
        own_kernel,
        grid=(steps,),
        in_specs=[
            pl.BlockSpec(both.shape, lambda j: (0, 0)),
            pl.BlockSpec(mine.shape, lambda j: (0, 0)),
            pl.BlockSpec((3, width, STEP_COLS), lambda j: (0, 0, jnp.minimum(j, half - 1))),
            pl.BlockSpec((3, width, STEP_COLS), lambda j: (0, 0, jnp.maximum(j - half, 0))),
        ],
        out_specs=[
            pl.BlockSpec((rows, STEP_COLS), lambda j: (0, j)),
            pl.BlockSpec((rows, STEP_COLS), lambda j: (0, j)),
            pl.BlockSpec((1, rows, LANES), lambda j: (j, 0, 0)),
        ],
        out_shape=[
            jax.ShapeDtypeStruct((rows, width), BF16),
            jax.ShapeDtypeStruct((rows, width), F32),
            jax.ShapeDtypeStruct((steps, rows, LANES), F32),
        ],
        name="own_attention",
    )(both, mine, w_own, w_other)


def block_kernel(
    place_ref,
    mask_ref,
    query_ref,
    rows_ref,
    key_own_ref,
    value_own_ref,
    key_other_ref,
    value_other_ref,
    acc_in,
    stats_in,
    acc_ref,
    stats_ref,
    *,
    distance,
    blocks,
):
    step = pl.program_id(0)
    half = pl.num_programs(0) // 2
    here = place_ref[0]
    source = jnp.where(place_ref[1] == 0, here - distance, here + distance)
    inside = (source >= 0) & (source < blocks)
    listed = mask_ref[here % 8, jnp.clip(source, 0, blocks - 1)]
    active = inside & (listed > 0)

    def work(w_key, w_value):
        attend_step(
            query_ref[...], rows_ref[...], w_key[0], w_value[0], stats_in, acc_in, stats_ref, acc_ref
        )

    @pl.when(active & (step < half))
    def _():
        work(key_own_ref, value_own_ref)

    @pl.when(active & (step >= half))
    def _():
        work(key_other_ref, value_other_ref)

    @pl.when(jnp.logical_not(active))
    def _():
        acc_ref[...] = acc_in[...]
        stats_ref[...] = stats_in[...]


def block_attention(place, block_mask, queries, rows, w_own, w_other, acc, stats, distance):
    count, width = queries.shape
    steps = width // STEP_COLS
    half = steps // 2
    blocks = block_mask.shape[0]

    def body(*refs):
        block_kernel(*refs, distance=distance, blocks=blocks)

    grid_spec = pltpu.PrefetchScalarGridSpec(
        num_scalar_prefetch=1,
        grid=(steps,),
        in_specs=[
            pl.BlockSpec((8, blocks), lambda j, s: (s[0] // 8, 0), memory_space=pltpu.SMEM),
            pl.BlockSpec((count, STEP_COLS), lambda j, s: (0, j)),
            pl.BlockSpec(rows.shape, lambda j, s: (0, 0)),
            pl.BlockSpec((1, width, STEP_COLS), lambda j, s: (1, 0, jnp.minimum(j, half - 1))),
            pl.BlockSpec((1, width, STEP_COLS), lambda j, s: (2, 0, jnp.minimum(j, half - 1))),
            pl.BlockSpec((1, width, STEP_COLS), lambda j, s: (1, 0, jnp.maximum(j - half, 0))),
            pl.BlockSpec((1, width, STEP_COLS), lambda j, s: (2, 0, jnp.maximum(j - half, 0))),
            pl.BlockSpec((count, STEP_COLS), lambda j, s: (0, j)),
            pl.BlockSpec((1, count, LANES), lambda j, s: (j, 0, 0)),
        ],
        out_specs=[
            pl.BlockSpec((count, STEP_COLS), lambda j, s: (0, j)),
            pl.BlockSpec((1, count, LANES), lambda j, s: (j, 0, 0)),
        ],
    )
    return pl.pallas_call(
        body,
        grid_spec=grid_spec,
        out_shape=[
            jax.ShapeDtypeStruct(acc.shape, F32),
            jax.ShapeDtypeStruct(stats.shape, F32),
        ],
        input_output_aliases={8: 0, 9: 1},
    )(place, block_mask, queries, rows, w_own, w_own, w_other, w_other, acc, stats)


def pack_kernel(place_ref, acc_ref, stats_ref, out_ref):
    steps = stats_ref.shape[0]
    width = acc_ref.shape[1]
    out_ref[:, :width] = acc_ref[...]
    for j in range(steps):
        out_ref[:, width + 8 * j : width + 8 * j + 8] = stats_ref[j, :, 0:8]
    out_ref[:, width + 8 * steps :] = jnp.zeros(
        (out_ref.shape[0], out_ref.shape[1] - width - 8 * steps), F32
    )


def pack(place, acc, stats):
    count, width = acc.shape
    half = count // 2
    steps = stats.shape[0]
    grid_spec = pltpu.PrefetchScalarGridSpec(
        num_scalar_prefetch=1,
        grid=(1,),
        in_specs=[
            pl.BlockSpec((half, width), lambda i, s: (1 - s[1], 0)),
            pl.BlockSpec((steps, half, LANES), lambda i, s: (0, 1 - s[1], 0)),
        ],
        out_specs=pl.BlockSpec((half, width + LANES), lambda i, s: (0, 0)),
    )
    return pl.pallas_call(
        pack_kernel,
        grid_spec=grid_spec,
        out_shape=jax.ShapeDtypeStruct((half, width + LANES), F32),
        name="pack",
    )(place, acc, stats)


def tail_kernel(
    place_ref,
    acc_ref,
    stats_ref,
    sent_ref,
    tokens_ref,
    w_out_own,
    w_out_other,
    gain_ref,
    bias_ref,
    w_up_own,
    w_up_other,
    w_down_own,
    w_down_other,
    out_ref,
    out_buf,
    up_buf,
    down_buf,
    out_sem,
    up_sem,
    down_sem,
):
    rows, width = tokens_ref.shape
    steps = stats_ref.shape[0]
    half = steps // 2
    chunk = up_buf.shape[2]
    hidden_half = w_up_own.shape[1]
    per_half = hidden_half // chunk

    copies_out = [
        pltpu.make_async_copy(source, out_buf.at[i], out_sem.at[i])
        for i, source in enumerate((w_out_own, w_out_other))
    ]
    copies_up = []
    copies_down = []
    for i, (up, down) in enumerate(((w_up_own, w_down_own), (w_up_other, w_down_other))):
        for j in range(per_half):
            k = i * per_half + j
            copies_up.append(
                pltpu.make_async_copy(
                    up.at[:, pl.ds(j * chunk, chunk)], up_buf.at[k], up_sem.at[k]
                )
            )
            copies_down.append(
                pltpu.make_async_copy(
                    down.at[pl.ds(j * chunk, chunk), :], down_buf.at[k], down_sem.at[k]
                )
            )
    for copy in copies_out:
        copy.start()
    for up, down in zip(copies_up, copies_down):
        up.start()
        down.start()

    first = lax.broadcasted_iota(jnp.int32, (rows, LANES), 1) < HDIM
    pieces = []
    for j in range(steps):
        other = (j + half) % steps
        for pair in range(STEP_COLS // LANES):
            mine = []
            theirs = []
            for head in range(2):
                lane = 4 * pair + head
                base = width + 8 * other + lane
                my_max = stats_ref[j, :, lane : lane + 1]
                my_sum = stats_ref[j, :, lane + 2 : lane + 3]
                their_max = sent_ref[:, base : base + 1]
                their_sum = sent_ref[:, base + 2 : base + 3]
                top = jnp.maximum(my_max, their_max)
                my_part = jnp.exp2(my_max - top)
                their_part = jnp.exp2(their_max - top)
                total = my_sum * my_part + their_sum * their_part
                mine.append(my_part / total)
                theirs.append(their_part / total)
            col = j * STEP_COLS + pair * LANES
            col_other = other * STEP_COLS + pair * LANES
            merged = acc_ref[:, col : col + LANES] * jnp.where(first, mine[0], mine[1])
            merged = merged + sent_ref[:, col_other : col_other + LANES] * jnp.where(
                first, theirs[0], theirs[1]
            )
            pieces.append(merged.astype(BF16))
    attended = jnp.concatenate(pieces, axis=1)
    for copy in copies_out:
        copy.wait()
    halfway = width // 2
    projected = dot(attended[:, :halfway], out_buf[0]) + dot(attended[:, halfway:], out_buf[1])
    resid = (tokens_ref[...].astype(F32) + projected).astype(BF16)
    normed = layer_norm(resid, gain_ref[...], bias_ref[...]).astype(BF16)
    total = resid.astype(F32)
    for k in range(2 * per_half):
        copies_up[k].wait()
        raised = dot(normed, up_buf[k])
        hidden = (raised * (1.0 + lax.erf(raised * (0.5**0.5))) * 0.5).astype(BF16)
        copies_down[k].wait()
        total = total + dot(hidden, down_buf[k])
    out_ref[...] = total.astype(BF16)


def tail(place, acc, stats, both_sent, tokens, w_out, w_out_other, gain, bias, w_up, w_up_other, w_down, w_down_other):
    rows, width = tokens.shape
    steps = stats.shape[0]
    hidden_half = w_up.shape[1]
    chunk = 512
    chunks = 2 * hidden_half // chunk
    whole = pl.BlockSpec(memory_space=pl.ANY)
    vector = pl.BlockSpec((1, width), lambda i, s: (0, 0))
    grid_spec = pltpu.PrefetchScalarGridSpec(
        num_scalar_prefetch=1,
        grid=(1,),
        in_specs=[
            pl.BlockSpec((rows, width), lambda i, s: (s[1], 0)),
            pl.BlockSpec((steps, rows, LANES), lambda i, s: (0, s[1], 0)),
            pl.BlockSpec((rows, width + LANES), lambda i, s: (0, 0)),
            pl.BlockSpec((rows, width), lambda i, s: (0, 0)),
            whole,
            whole,
            vector,
            vector,
            whole,
            whole,
            whole,
            whole,
        ],
        out_specs=pl.BlockSpec((rows, width), lambda i, s: (0, 0)),
        scratch_shapes=[
            pltpu.VMEM((2, width // 2, width), BF16),
            pltpu.VMEM((chunks, width, chunk), BF16),
            pltpu.VMEM((chunks, chunk, width), BF16),
            pltpu.SemaphoreType.DMA((2,)),
            pltpu.SemaphoreType.DMA((chunks,)),
            pltpu.SemaphoreType.DMA((chunks,)),
        ],
    )
    return pl.pallas_call(
        tail_kernel,
        grid_spec=grid_spec,
        out_shape=jax.ShapeDtypeStruct(tokens.shape, BF16),
        name="tail",
    )(
        place,
        acc,
        stats,
        both_sent,
        tokens,
        w_out,
        w_out_other,
        gain.reshape(1, -1),
        bias.reshape(1, -1),
        w_up,
        w_up_other,
        w_down,
        w_down_other,
    )


def from_partner(array):
    return lax.ppermute(array, "head", [(0, 1), (1, 0)])


def from_block(array, distance):
    blocks = lax.axis_size("seq")
    ahead = [(2 * i, 2 * (i + distance)) for i in range(blocks - distance)]
    behind = [(2 * i + 1, 2 * (i - distance) + 1) for i in range(distance, blocks)]
    return lax.ppermute(array, ("seq", "head"), ahead + behind)


def shards(tokens, ln1_gain, ln1_bias, w_qkv, w_out, ln2_gain, ln2_bias, w_up, w_down, block_mask):
    here = lax.axis_index("seq")
    core = lax.axis_index("head")
    place = jnp.stack([here, core]).astype(jnp.int32)
    w_own = jnp.transpose(w_qkv, (1, 0, 2))
    mine = norm_rows(tokens, ln1_gain, ln1_bias)
    both = lax.all_gather(mine, "head", axis=0, tiled=True)
    near = {}
    for d in range(1, REACH + 1):
        near[d] = from_block(both, d)
    w_other = from_partner(w_own)
    w_out_other = from_partner(w_out)
    w_up_other = from_partner(w_up)
    w_down_other = from_partner(w_down)
    queries, acc, stats = own_attention(both, mine, w_own, w_other)
    for d in (1, 3, 4, 2):
        acc, stats = block_attention(
            place, block_mask, queries, near[d], w_own, w_other, acc, stats, d
        )
    packed = pack(place, acc, stats)
    sent = from_partner(packed)
    return tail(
        place,
        acc,
        stats,
        sent,
        tokens,
        w_out,
        w_out_other,
        ln2_gain,
        ln2_bias,
        w_up,
        w_up_other,
        w_down,
        w_down_other,
    )


def solution(mesh):
    in_specs = (
        P(("seq", "head"), None),
        P(),
        P(),
        P(None, None, "head"),
        P("head", None),
        P(),
        P(),
        P(None, "head"),
        P("head", None),
        P(),
    )
    out_specs = P(("seq", "head"), None)
    return jax.shard_map(
        shards, mesh=mesh, in_specs=in_specs, out_specs=out_specs, check_vma=False
    )
```

time: 200 us -> 155 us (0.78)
  the two profiles are of different devices: /device:TPU:1 before, /device:TPU:27 now
where the time goes in v1:
time: 155 us; the launch traced here: 154 us
  Pallas kernels  102 us (66%)
  starting transfers between devices  25.1 us (16%)
  waiting for transfers between devices  13.8 us (9%)
  blocking collectives  11.7 us (8%)
    pallas_call x4, Pallas kernels, block_attention(): pl.pallas_call(body, grid_spec=grid_spec, out_shape=[jax.ShapeDtypeStruct...  76 us
    ppermute x5, starting transfers between devices, from_partner(): return lax.ppermute(array, 'head', [(0, 1), (1, 0)])  15.9 us
    pallas_call x1, Pallas kernels, tail(): pl.pallas_call(tail_kernel, grid_spec=grid_spec, out_shape=jax.ShapeDtype...  14.1 us
    ppermute x4, waiting for transfers between devices, from_block(): return lax.ppermute(array, ('seq', 'head'), ahead + behind)  11.9 us
    all_gather x1, blocking collectives, shards(): both = lax.all_gather(mine, 'head', axis=0, tiled=True)  11.7 us
    ppermute x4, starting transfers between devices, from_block(): return lax.ppermute(array, ('seq', 'head'), ahead + behind)  9.13 us
    pallas_call x1, Pallas kernels, own_attention(): pl.pallas_call(own_kernel, grid=(steps,), in_specs=[pl.BlockSpec(both.sha...  7.23 us
  transfers between devices with their start and end apart: 9, of which 3 were waited for; matrix products, arithmetic and copies ran while one was open for 0% of the time, Pallas kernels for 57%

profile of v1, /device:TPU:27, one launch (start us, length us, event | category | flops | bytes accessed | tf_op | source)
XLA Modules:
  0.0 154.4 jit_solution(6638414641030298436)
XLA Ops:
  0.0 2.6 %collective-permute-start = (bf16[3,1024,512]{2,1,0:T(8,128)(2,1)}, bf16[3,1024,512]{2,1,0:T(8,128)(2,1)S(1)}, u32[]{:S(2)}, u32[]{:S(2)}) collective-permute-start(bf16[3,1024,512]{2,1,0:T(8,128)(2,1)} %bitcast.7), channel_id=1, source_target_pairs={{0,1},{1,0},{2,3},{3,2},{4,5},{5,4},{6,7},{7,6},{8,9},{9,8},{10,11... | collective-permute-start | bytes 9437192 | tf_op jit(solution)/shard_map/ppermute | solution.py:418
  2.6 1.9 %collective-permute-start.7 = (bf16[1024,2048]{1,0:T(8,128)(2,1)}, bf16[1024,2048]{1,0:T(8,128)(2,1)}, u32[]{:S(2)}, u32[]{:S(2)}) collective-permute-start(bf16[1024,2048]{1,0:T(8,128)(2,1)} %w_up_own.1), channel_id=1, source_target_pairs={{0,1},{1,0},{2,3},{3,2},{4,5},{5,4},{6,7},{7,6},{8,9},{9,8},{10,11... | collective-permute-start | bytes 12582920 | tf_op jit(solution)/shard_map/ppermute | solution.py:418
  4.5 2.4 %collective-permute-start.8 = (bf16[2048,1024]{1,0:T(8,128)(2,1)}, bf16[2048,1024]{1,0:T(8,128)(2,1)}, u32[]{:S(2)}, u32[]{:S(2)}) collective-permute-start(bf16[2048,1024]{1,0:T(8,128)(2,1)} %w_down_own.1), channel_id=1, source_target_pairs={{0,1},{1,0},{2,3},{3,2},{4,5},{5,4},{6,7},{7,6},{8,9},{9,8},{10,11... | collective-permute-start | bytes 12582920 | tf_op jit(solution)/shard_map/ppermute | solution.py:418
  6.9 1.9 %norm_rows.1.mine_ref = bf16[128,1024]{1,0:T(8,128)(2,1)} custom-call(bf16[128,1024]{1,0:T(8,128)(2,1)} %tokens_ref.3, f32[1,1024]{1,0:T(1,128)} %bitcast.17, f32[1,1024]{1,0:T(1,128)} %bitcast.18), custom_call_target="tpu_custom_call" | custom-call | tf_op jit(solution)/shard_map/norm_rows/pallas_call | solution.py:38
  8.9 11.7 %all_gather.3.both_ref = bf16[256,1024]{1,0:T(8,128)(2,1)} all-gather(bf16[128,1024]{1,0:T(8,128)(2,1)} %norm_rows.1.mine_ref), channel_id=1, replica_groups=mesh['seq'=256,'head'=2] {'head'}, dimensions={0}, use_global_device_ids=true | all-gather | bytes 786432 | tf_op jit(solution)/shard_map/all_gather | solution.py:434
  20.6 2.2 %collective-permute-start.4 = (bf16[256,1024]{1,0:T(8,128)(2,1)}, bf16[256,1024]{1,0:T(8,128)(2,1)S(1)}, u32[]{:S(2)}, u32[]{:S(2)}) collective-permute-start(bf16[256,1024]{1,0:T(8,128)(2,1)} %all_gather.3.both_ref), channel_id=1, source_target_pairs={{0,2},{2,4},{4,6},{6,8},{8,10},{10,12},{12,14},{14,16},{16,18},{18... | collective-permute-start | bytes 1572872 | tf_op jit(solution)/shard_map/ppermute | solution.py:425
  22.7 3.0 %collective-permute-start.3 = (bf16[256,1024]{1,0:T(8,128)(2,1)}, bf16[256,1024]{1,0:T(8,128)(2,1)S(1)}, u32[]{:S(2)}, u32[]{:S(2)}) collective-permute-start(bf16[256,1024]{1,0:T(8,128)(2,1)} %all_gather.3.both_ref), channel_id=1, source_target_pairs={{0,6},{2,8},{4,10},{6,12},{8,14},{10,16},{12,18},{14,20},{16,22},{... | collective-permute-start | bytes 1572872 | tf_op jit(solution)/shard_map/ppermute | solution.py:425
  25.7 10.6 %collective-permute-done.4.refs_3_ = bf16[256,1024]{1,0:T(8,128)(2,1)S(1)} collective-permute-done((bf16[256,1024]{1,0:T(8,128)(2,1)}, bf16[256,1024]{1,0:T(8,128)(2,1)S(1)}, u32[]{:S(2)}, u32[]{:S(2)}) %collective-permute-start.4) | collective-permute-done | bytes 524320 | tf_op jit(solution)/shard_map/ppermute | solution.py:425
  36.3 0.0 copy-start.3
  36.3 2.1 %collective-permute-start.2 = (bf16[256,1024]{1,0:T(8,128)(2,1)}, bf16[256,1024]{1,0:T(8,128)(2,1)}, u32[]{:S(2)}, u32[]{:S(2)}) collective-permute-start(bf16[256,1024]{1,0:T(8,128)(2,1)} %all_gather.3.both_ref), channel_id=1, source_target_pairs={{0,8},{2,10},{4,12},{6,14},{8,16},{10,18},{12,20},{14,22},{16,24},... | collective-permute-start | bytes 1572872 | tf_op jit(solution)/shard_map/ppermute | solution.py:425
  38.4 1.3 collective-permute-done.3.refs_3_
  39.7 0.0 copy-start.2
  39.7 1.9 %collective-permute-start.1 = (bf16[256,1024]{1,0:T(8,128)(2,1)}, bf16[256,1024]{1,0:T(8,128)(2,1)}, u32[]{:S(2)}, u32[]{:S(2)}) collective-permute-start(bf16[256,1024]{1,0:T(8,128)(2,1)} %all_gather.3.both_ref), channel_id=1, source_target_pairs={{0,4},{2,6},{4,8},{6,10},{8,12},{10,14},{12,16},{14,18},{16,20},{1... | collective-permute-start | bytes 1572872 | tf_op jit(solution)/shard_map/ppermute | solution.py:425
  41.6 0.0 collective-permute-done.w_other_ref.refs_6_.refs_7_
  41.6 0.0 copy-done.2
  41.6 0.0 copy-start
  41.6 6.9 %collective-permute-start.6 = (bf16[512,1024]{1,0:T(8,128)(2,1)}, bf16[512,1024]{1,0:T(8,128)(2,1)}, u32[]{:S(2)}, u32[]{:S(2)}) collective-permute-start(bf16[512,1024]{1,0:T(8,128)(2,1)} %w_out_own.1), channel_id=1, source_target_pairs={{0,1},{1,0},{2,3},{3,2},{4,5},{5,4},{6,7},{7,6},{8,9},{9,8},{10,11... | collective-permute-start | bytes 3145736 | tf_op jit(solution)/shard_map/ppermute | solution.py:418
  48.5 0.0 copy-done.3
  48.5 0.6 pad_add_fusion.refs_0_.place_ref
  49.2 0.0 copy-done
  49.2 7.2 %own_attention.1 = (bf16[256,1024]{1,0:T(8,128)(2,1)}, f32[256,1024]{1,0:T(8,128)}, f32[4,256,128]{2,1,0:T(8,128)}) custom-call(bf16[256,1024]{1,0:T(8,128)(2,1)} %all_gather.3.both_ref, bf16[128,1024]{1,0:T(8,128)(2,1)} %norm_rows.1.mine_ref, bf16[3,1024,512]{2,1,0:T(8,128)(2,1)} %bitcast.8, bf16[3,1024,512]{2,1,0:T(8,128)(2,1)} %copy-done), custom_call_target="tpu_custom_call" | custom-call | tf_op jit(solution)/shard_map/own_attention/pallas_call | solution.py:124
  56.4 18.9 %shard_map.100 = (f32[256,1024]{1,0:T(8,128)}, f32[4,256,128]{2,1,0:T(8,128)}) custom-call(s32[2]{0:T(128)} %pad_add_fusion.refs_0_.place_ref, s32[256,256]{1,0:T(8,128)} %refs_1_.7, bf16[256,1024]{1,0:T(8,128)(2,1)} %get-tuple-element.16.refs_2_, bf16[256,1024]{1,0:T(8,128)(2,1)} %copy-done.3, ...), custom_call_target="tpu_custom_call", output_to_operand_aliasing={{0}: (8, {}), {1}: (9, {})} | custom-call | tf_op jit(solution)/shard_map/pallas_call | solution.py:219
  75.4 18.9 %shard_map.101 = (f32[256,1024]{1,0:T(8,128)}, f32[4,256,128]{2,1,0:T(8,128)}) custom-call(s32[2]{0:T(128)} %pad_add_fusion.refs_0_.place_ref, s32[256,256]{1,0:T(8,128)} %refs_1_.7, bf16[256,1024]{1,0:T(8,128)(2,1)} %get-tuple-element.16.refs_2_, bf16[256,1024]{1,0:T(8,128)(2,1)} %copy-done.2, ...), custom_call_target="tpu_custom_call", output_to_operand_aliasing={{0}: (8, {}), {1}: (9, {})} | custom-call | tf_op jit(solution)/shard_map/pallas_call | solution.py:219
  94.3 0.0 collective-permute-done.2.refs_3_
  94.3 19.1 %shard_map.102 = (f32[256,1024]{1,0:T(8,128)}, f32[4,256,128]{2,1,0:T(8,128)}) custom-call(s32[2]{0:T(128)} %pad_add_fusion.refs_0_.place_ref, s32[256,256]{1,0:T(8,128)} %refs_1_.7, bf16[256,1024]{1,0:T(8,128)(2,1)} %get-tuple-element.16.refs_2_, bf16[256,1024]{1,0:T(8,128)(2,1)} %collective-permute-done.2.refs_3_, ...), custom_call_target="tpu_custom_call", output_to_operand_aliasing={{0}: (8, {}), {1}: (9, {})} | custom-call | tf_op jit(solution)/shard_map/pallas_call | solution.py:219
  113.5 0.0 collective-permute-done.1.refs_3_
  113.5 19.0 %shard_map.103 = (f32[256,1024]{1,0:T(8,128)}, f32[4,256,128]{2,1,0:T(8,128)}) custom-call(s32[2]{0:T(128)} %pad_add_fusion.refs_0_.place_ref, s32[256,256]{1,0:T(8,128)} %refs_1_.7, bf16[256,1024]{1,0:T(8,128)(2,1)} %get-tuple-element.16.refs_2_, bf16[256,1024]{1,0:T(8,128)(2,1)} %collective-permute-done.1.refs_3_, ...), custom_call_target="tpu_custom_call", output_to_operand_aliasing={{0}: (8, {}), {1}: (9, {})} | custom-call | tf_op jit(solution)/shard_map/pallas_call | solution.py:219
  132.4 2.8 %pack.1 = f32[128,1152]{1,0:T(8,128)} custom-call(s32[2]{0:T(128)} %pad_add_fusion.refs_0_.place_ref, f32[256,1024]{1,0:T(8,128)} %get-tuple-element.25.acc_ref, f32[4,256,128]{2,1,0:T(8,128)} %get-tuple-element.26.stats_ref), custom_call_target="tpu_custom_call" | custom-call | tf_op jit(solution)/shard_map/pack/pallas_call | solution.py:254
  135.2 2.1 %collective-permute-start.5 = (f32[128,1152]{1,0:T(8,128)}, f32[128,1152]{1,0:T(8,128)S(1)}, u32[]{:S(2)}, u32[]{:S(2)}) collective-permute-start(f32[128,1152]{1,0:T(8,128)} %pack.1), channel_id=1, source_target_pairs={{0,1},{1,0},{2,3},{3,2},{4,5},{5,4},{6,7},{7,6},{8,9},{9,8},{10,11... | collective-permute-start | bytes 1769480 | tf_op jit(solution)/shard_map/ppermute | solution.py:418
  137.3 0.0 collective-permute-done.6.w_out_other
  137.3 1.9 %collective-permute-done.5.sent_ref = f32[128,1152]{1,0:T(8,128)S(1)} collective-permute-done((f32[128,1152]{1,0:T(8,128)}, f32[128,1152]{1,0:T(8,128)S(1)}, u32[]{:S(2)}, u32[]{:S(2)}) %collective-permute-start.5) | collective-permute-done | bytes 589856 | tf_op jit(solution)/shard_map/ppermute | solution.py:418
  139.3 0.0 copy-start.1
  139.3 0.0 collective-permute-done.7.w_up_other
  139.3 0.0 collective-permute-done.8.w_down_other
  139.3 0.9 copy-done.1
  140.1 14.1 %tail.1 = bf16[128,1024]{1,0:T(8,128)(2,1)} custom-call(s32[2]{0:T(128)} %pad_add_fusion.refs_0_.place_ref, f32[256,1024]{1,0:T(8,128)} %get-tuple-element.25.acc_ref, f32[4,256,128]{2,1,0:T(8,128)} %get-tuple-element.26.stats_ref, f32[128,1152]{1,0:T(8,128)} %copy-done.1, bf16[128,1024]{1,0:T(8,128)(2,1)} %tokens_ref.3, bf16[512,1024]{1,0:T(8,128)(2,1)} %w_out_own.1, ...), custom_call_target="tpu_custom_call" | custom-call | tf_op jit(solution)/shard_map/tail/pallas_call | solution.py:395
Async XLA Ops:
  0.0 41.6 %collective-permute-start = (bf16[3,1024,512]{2,1,0:T(8,128)(2,1)}, bf16[3,1024,512]{2,1,0:T(8,128)(2,1)S(1)}, u32[]{:S(2)}, u32[]{:S(2)}) collective-permute-start(bf16[3,1024,512]{2,1,0:T(8,128)(2,1)} %bitcast.7), channel_id=1, source_target_pairs={{0,1},{1,0},{2,3},{3,2},{4,5},{5,4},{6,7},{7,6},{8,9},{9,8},{10,11... | collective-permute-start | bytes 9437192 | tf_op jit(solution)/shard_map/ppermute | solution.py:418
  2.6 136.7 %collective-permute-start.7 = (bf16[1024,2048]{1,0:T(8,128)(2,1)}, bf16[1024,2048]{1,0:T(8,128)(2,1)}, u32[]{:S(2)}, u32[]{:S(2)}) collective-permute-start(bf16[1024,2048]{1,0:T(8,128)(2,1)} %w_up_own.1), channel_id=1, source_target_pairs={{0,1},{1,0},{2,3},{3,2},{4,5},{5,4},{6,7},{7,6},{8,9},{9,8},{10,11... | collective-permute-start | bytes 12582920 | tf_op jit(solution)/shard_map/ppermute | solution.py:418
  4.5 134.8 %collective-permute-start.8 = (bf16[2048,1024]{1,0:T(8,128)(2,1)}, bf16[2048,1024]{1,0:T(8,128)(2,1)}, u32[]{:S(2)}, u32[]{:S(2)}) collective-permute-start(bf16[2048,1024]{1,0:T(8,128)(2,1)} %w_down_own.1), channel_id=1, source_target_pairs={{0,1},{1,0},{2,3},{3,2},{4,5},{5,4},{6,7},{7,6},{8,9},{9,8},{10,11... | collective-permute-start | bytes 12582920 | tf_op jit(solution)/shard_map/ppermute | solution.py:418
  20.6 15.7 %collective-permute-start.4 = (bf16[256,1024]{1,0:T(8,128)(2,1)}, bf16[256,1024]{1,0:T(8,128)(2,1)S(1)}, u32[]{:S(2)}, u32[]{:S(2)}) collective-permute-start(bf16[256,1024]{1,0:T(8,128)(2,1)} %all_gather.3.both_ref), channel_id=1, source_target_pairs={{0,2},{2,4},{4,6},{6,8},{8,10},{10,12},{12,14},{14,16},{16,18},{18... | collective-permute-start | bytes 1572872 | tf_op jit(solution)/shard_map/ppermute | solution.py:425
  22.7 17.0 %collective-permute-start.3 = (bf16[256,1024]{1,0:T(8,128)(2,1)}, bf16[256,1024]{1,0:T(8,128)(2,1)S(1)}, u32[]{:S(2)}, u32[]{:S(2)}) collective-permute-start(bf16[256,1024]{1,0:T(8,128)(2,1)} %all_gather.3.both_ref), channel_id=1, source_target_pairs={{0,6},{2,8},{4,10},{6,12},{8,14},{10,16},{12,18},{14,20},{16,22},{... | collective-permute-start | bytes 1572872 | tf_op jit(solution)/shard_map/ppermute | solution.py:425
  36.3 12.2 %copy-start.3 = (bf16[256,1024]{1,0:T(8,128)(2,1)}, bf16[256,1024]{1,0:T(8,128)(2,1)S(1)}, u32[]{:S(2)}) copy-start(bf16[256,1024]{1,0:T(8,128)(2,1)S(1)} %collective-permute-done.4.refs_3_) | copy-start | bytes 1572868
  36.3 58.0 %collective-permute-start.2 = (bf16[256,1024]{1,0:T(8,128)(2,1)}, bf16[256,1024]{1,0:T(8,128)(2,1)}, u32[]{:S(2)}, u32[]{:S(2)}) collective-permute-start(bf16[256,1024]{1,0:T(8,128)(2,1)} %all_gather.3.both_ref), channel_id=1, source_target_pairs={{0,8},{2,10},{4,12},{6,14},{8,16},{10,18},{12,20},{14,22},{16,24},... | collective-permute-start | bytes 1572872 | tf_op jit(solution)/shard_map/ppermute | solution.py:425
  39.7 1.9 %copy-start.2 = (bf16[256,1024]{1,0:T(8,128)(2,1)}, bf16[256,1024]{1,0:T(8,128)(2,1)S(1)}, u32[]{:S(2)}) copy-start(bf16[256,1024]{1,0:T(8,128)(2,1)S(1)} %collective-permute-done.3.refs_3_) | copy-start | bytes 1572868
  39.7 73.8 %collective-permute-start.1 = (bf16[256,1024]{1,0:T(8,128)(2,1)}, bf16[256,1024]{1,0:T(8,128)(2,1)}, u32[]{:S(2)}, u32[]{:S(2)}) collective-permute-start(bf16[256,1024]{1,0:T(8,128)(2,1)} %all_gather.3.both_ref), channel_id=1, source_target_pairs={{0,4},{2,6},{4,8},{6,10},{8,12},{10,14},{12,16},{14,18},{16,20},{1... | collective-permute-start | bytes 1572872 | tf_op jit(solution)/shard_map/ppermute | solution.py:425
  41.6 7.6 %copy-start = (bf16[3,1024,512]{2,1,0:T(8,128)(2,1)}, bf16[3,1024,512]{2,1,0:T(8,128)(2,1)S(1)}, u32[]{:S(2)}) copy-start(bf16[3,1024,512]{2,1,0:T(8,128)(2,1)S(1)} %collective-permute-done.w_other_ref.refs_6_.refs_7_) | copy-start | bytes 9437188
  41.6 95.7 %collective-permute-start.6 = (bf16[512,1024]{1,0:T(8,128)(2,1)}, bf16[512,1024]{1,0:T(8,128)(2,1)}, u32[]{:S(2)}, u32[]{:S(2)}) collective-permute-start(bf16[512,1024]{1,0:T(8,128)(2,1)} %w_out_own.1), channel_id=1, source_target_pairs={{0,1},{1,0},{2,3},{3,2},{4,5},{5,4},{6,7},{7,6},{8,9},{9,8},{10,11... | collective-permute-start | bytes 3145736 | tf_op jit(solution)/shard_map/ppermute | solution.py:418
  135.2 4.1 %collective-permute-start.5 = (f32[128,1152]{1,0:T(8,128)}, f32[128,1152]{1,0:T(8,128)S(1)}, u32[]{:S(2)}, u32[]{:S(2)}) collective-permute-start(f32[128,1152]{1,0:T(8,128)} %pack.1), channel_id=1, source_target_pairs={{0,1},{1,0},{2,3},{3,2},{4,5},{5,4},{6,7},{7,6},{8,9},{9,8},{10,11... | collective-permute-start | bytes 1769480 | tf_op jit(solution)/shard_map/ppermute | solution.py:418
  139.3 0.9 copy-start.1

commit v2 on v0

v2 whole, which is shorter than its diff:
```python
import math

import jax
import jax.numpy as jnp
from jax import lax
from jax.experimental import pallas as pl
from jax.experimental.pallas import tpu as pltpu
from jax.sharding import PartitionSpec as P


HDIM = 64
REACH = 4
LANES = 128
STEP_COLS = 256
EXP_SCALE = HDIM ** (-0.5) * math.log2(math.e)
F32 = jnp.float32
BF16 = jnp.bfloat16

norm_eps = 1e-06


def layer_norm(inputs, gain, shift):
    inputs = inputs.astype(F32)
    center = inputs - jnp.mean(inputs, axis=-1, keepdims=True)
    spread = jnp.mean(center * center, axis=-1, keepdims=True)
    return center * lax.rsqrt(spread + norm_eps) * gain + shift


def dot(left, right):
    return jnp.dot(left, right, preferred_element_type=F32)


def held(array):
    return pltpu.with_memory_space_constraint(array, pltpu.VMEM)


def in_hbm(array):
    return pltpu.with_memory_space_constraint(array, pltpu.HBM)


def in_vmem():
    return pl.BlockSpec(memory_space=pltpu.VMEM)


def vmem_out(shape, dtype):
    return pltpu.VMEM(shape, dtype)


def params(mib):
    return pltpu.CompilerParams(vmem_limit_bytes=mib * 1024 * 1024)


def norm_kernel(here_ref, core_ref, tokens_ref, gain_ref, bias_ref, out_ref):
    out_ref[...] = layer_norm(tokens_ref[...], gain_ref[...], bias_ref[...]).astype(BF16)


def norm_rows(place, tokens, gain, bias):
    rows, width = tokens.shape
    vector = pl.BlockSpec((1, width), lambda i, s, c: (0, 0))
    whole = pl.BlockSpec((rows, width), lambda i, s, c: (0, 0))
    grid_spec = pltpu.PrefetchScalarGridSpec(
        num_scalar_prefetch=2, grid=(1,), in_specs=[whole, vector, vector], out_specs=whole
    )
    return pl.pallas_call(
        norm_kernel,
        grid_spec=grid_spec,
        out_shape=jax.ShapeDtypeStruct(tokens.shape, BF16),
        name="norm_rows",
    )(*place, tokens, gain.reshape(1, -1), bias.reshape(1, -1))


def attend_heads(keys, values_t, query_ref, pair, acc_ref, stats_ref, fresh):
    count = query_ref.shape[2] // 2
    scores = dot(keys, query_ref[pair])
    top = jnp.max(scores, axis=0, keepdims=True)
    old_top = stats_ref[pair, 0:1, :]
    if not fresh:
        top = jnp.maximum(top, old_top)
    weights = jnp.exp2((scores - top) * EXP_SCALE)
    total = jnp.sum(weights, axis=0, keepdims=True)
    low = weights.astype(BF16)
    if not fresh:
        decay = jnp.exp2((old_top - top) * EXP_SCALE)
        total = total + stats_ref[pair, 1:2, :] * decay
    stats_ref[pair, 0:1, :] = top
    stats_ref[pair, 1:2, :] = total
    for head in range(2):
        lanes = slice(head * count, (head + 1) * count)
        rows = slice((2 * pair + head) * HDIM, (2 * pair + head + 1) * HDIM)
        mixture = dot(values_t[head * HDIM : (head + 1) * HDIM], low[:, lanes])
        if not fresh:
            mixture = mixture + acc_ref[rows, :] * decay[:, lanes]
        acc_ref[rows, :] = mixture


def attend_rows(rows, w_pair, query_ref, acc_ref, stats_ref, fresh):
    per_step = STEP_COLS // LANES
    pair = 0
    for weights in w_pair:
        for start in range(0, weights.shape[2], STEP_COLS):
            cols = slice(start, start + STEP_COLS)
            keys = dot(rows, weights[1, :, cols]).astype(BF16)
            values_t = dot(rows, weights[2, :, cols]).astype(BF16).T
            for i in range(per_step):
                part = slice(i * LANES, (i + 1) * LANES)
                attend_heads(
                    keys[:, part], values_t[part], query_ref, pair, acc_ref, stats_ref, fresh
                )
                pair += 1


def own_kernel(
    both_ref, mine_ref, w_own_hbm, w_other_ref, query_ref, acc_ref, stats_ref, w_own_ref, sems
):
    count = both_ref.shape[0]
    copies = [
        pltpu.make_async_copy(w_own_hbm.at[i], w_own_ref.at[i], sems.at[i]) for i in range(3)
    ]
    for copy in copies:
        copy.start()
    both = both_ref[...]
    pairs = acc_ref.shape[0] // LANES
    per_step = STEP_COLS // LANES
    halves = ((w_other_ref, pairs // 2), (w_own_ref, 0))
    for weights, pair in halves:
        if weights is w_own_ref:
            copies[0].wait()
        for start in range(0, weights.shape[2], STEP_COLS):
            queries_t = dot(both, weights[0, :, start : start + STEP_COLS]).astype(BF16).T
            for i in range(per_step):
                zero = jnp.zeros((HDIM, count), BF16)
                row = i * LANES
                query_ref[pair, :HDIM, :count] = queries_t[row : row + HDIM]
                query_ref[pair, :HDIM, count:] = zero
                query_ref[pair, HDIM:, :count] = zero
                query_ref[pair, HDIM:, count:] = queries_t[row + HDIM : row + LANES]
                pair += 1
    copies[1].wait()
    copies[2].wait()
    attend_rows(mine_ref[...], (w_own_ref, w_other_ref), query_ref, acc_ref, stats_ref, True)


def own_attention(both, mine, w_own, w_other):
    count, width = both.shape
    pairs = width // LANES
    return pl.pallas_call(
        own_kernel,
        in_specs=[in_vmem(), in_vmem(), pl.BlockSpec(memory_space=pl.ANY), in_vmem()],
        out_specs=[in_vmem()] * 4,
        out_shape=[
            vmem_out((pairs, LANES, 2 * count), BF16),
            vmem_out((width, count), F32),
            vmem_out((pairs, 8, 2 * count), F32),
            vmem_out(w_own.shape, BF16),
        ],
        scratch_shapes=[pltpu.SemaphoreType.DMA((3,))],
        compiler_params=params(6),
        name="own_attention",
    )(held(both), held(mine), in_hbm(w_own), held(w_other))


def block_kernel(*refs, distances, loads):
    near = len(distances)
    here_ref, core_ref, mask_ref, query_ref, w_own_ref, w_other_ref = refs[:6]
    rows_refs = refs[6 : 6 + near]
    sources = refs[6 + near : 6 + near + loads]
    acc_ref, stats_ref = refs[8 + near + loads : 10 + near + loads]
    targets = refs[10 + near + loads : 10 + near + 2 * loads]
    sems = refs[10 + near + 2 * loads]
    copies = [
        pltpu.make_async_copy(source, target, sems.at[i])
        for i, (source, target) in enumerate(zip(sources, targets))
    ]
    for copy in copies:
        copy.start()
    here = here_ref[0]
    blocks = mask_ref.shape[1]
    for distance, rows_ref in zip(distances, rows_refs):
        source = jnp.where(core_ref[0] == 0, here - distance, here + distance)
        inside = (source >= 0) & (source < blocks)
        listed = mask_ref[here % 8, jnp.clip(source, 0, blocks - 1)]

        @pl.when(inside & (listed > 0))
        def _(rows_ref=rows_ref):
            attend_rows(
                rows_ref[...], (w_own_ref, w_other_ref), query_ref, acc_ref, stats_ref, False
            )

    for copy in copies:
        copy.wait()


def block_attention(place, block_mask, queries, w_own, w_other, near, acc, stats, loaded):
    blocks = block_mask.shape[0]
    distances = tuple(d for d, _ in near)
    count = len(near)
    loads = len(loaded)

    def body(*refs):
        block_kernel(*refs, distances=distances, loads=loads)

    grid_spec = pltpu.PrefetchScalarGridSpec(
        num_scalar_prefetch=2,
        grid=(1,),
        in_specs=[
            pl.BlockSpec((8, blocks), lambda j, s, c: (s[0] // 8, 0), memory_space=pltpu.SMEM),
        ]
        + [in_vmem()] * (3 + count)
        + [pl.BlockSpec(memory_space=pl.ANY)] * loads
        + [in_vmem()] * 2,
        out_specs=[in_vmem()] * (2 + loads),
        scratch_shapes=[pltpu.SemaphoreType.DMA((loads,))],
    )
    at = 6 + count + loads
    outs = pl.pallas_call(
        body,
        grid_spec=grid_spec,
        out_shape=[vmem_out(acc.shape, F32), vmem_out(stats.shape, F32)]
        + [vmem_out(array.shape, BF16) for array in loaded],
        input_output_aliases={at: 0, at + 1: 1},
        compiler_params=params(6),
        name="block_attention",
    )(
        *place,
        block_mask,
        held(queries),
        held(w_own),
        held(w_other),
        *[held(rows) for _, rows in near],
        *[in_hbm(array) for array in loaded],
        held(acc),
        held(stats),
    )
    return outs[0], outs[1], outs[2:]


def pack_kernel(here_ref, core_ref, acc_ref, stats_ref, out_ref, keep_ref, level_ref, log_ref):
    half = out_ref.shape[1]
    count = 2 * half
    width = acc_ref.shape[0]
    pairs = stats_ref.shape[0]
    mine = core_ref[0]
    away = pl.ds(pl.multiple_of((1 - mine) * half, half), half)
    near = pl.ds(pl.multiple_of(mine * half, half), half)
    row = width
    for pair in range(pairs):
        for head in range(2):
            rows = slice((2 * pair + head) * HDIM, (2 * pair + head + 1) * HDIM)
            lanes = slice(head * count, (head + 1) * count)
            total = stats_ref[pair, 1:2, lanes]
            log_ref[0:1, :] = stats_ref[pair, 0:1, lanes] * EXP_SCALE + jnp.log2(total)
            log_ref[1:2, :] = 1.0 / total
            keep_ref[rows, :] = acc_ref[rows, near] * log_ref[1:2, near]
            level_ref[2 * pair + head : 2 * pair + head + 1, :] = log_ref[0:1, near]
            level = log_ref[0:1, away]
            out_ref[rows, :] = (acc_ref[rows, away] * log_ref[1:2, away]).astype(BF16)
            first = level.astype(BF16).astype(F32)
            second = (level - first).astype(BF16).astype(F32)
            third = level - first - second
            pieces = jnp.concatenate([first, second, third, jnp.zeros((13, half), F32)], axis=0)
            out_ref[row : row + 16, :] = pieces.astype(BF16)
            row += 16


def pack(place, acc, stats):
    width, count = acc.shape
    half = count // 2
    heads = 2 * stats.shape[0]
    rows = width + 16 * heads
    grid_spec = pltpu.PrefetchScalarGridSpec(
        num_scalar_prefetch=2,
        grid=(1,),
        in_specs=[in_vmem()] * 2,
        out_specs=[
            pl.BlockSpec((rows, half), lambda i, s, c: (0, 0)),
            pl.BlockSpec((width, half), lambda i, s, c: (0, 0)),
            pl.BlockSpec((heads, half), lambda i, s, c: (0, 0)),
        ],
        scratch_shapes=[pltpu.VMEM((8, count), F32)],
    )
    return pl.pallas_call(
        pack_kernel,
        grid_spec=grid_spec,
        out_shape=[
            jax.ShapeDtypeStruct((rows, half), BF16),
            jax.ShapeDtypeStruct((width, half), F32),
            jax.ShapeDtypeStruct((heads, half), F32),
        ],
        compiler_params=params(6),
        name="pack",
    )(*place, held(acc), held(stats))


def tail_kernel(
    here_ref,
    core_ref,
    sent_ref,
    keep_ref,
    level_ref,
    tokens_ref,
    gain_ref,
    bias_ref,
    w_out_own,
    w_out_other,
    w_up_own,
    w_up_other,
    w_down_own,
    w_down_other,
    out_ref,
):
    _, width = tokens_ref.shape
    heads = level_ref.shape[0]
    pieces = []
    for head in range(heads):
        other = (head + heads // 2) % heads
        rows = slice(head * HDIM, (head + 1) * HDIM)
        other_rows = slice(other * HDIM, (other + 1) * HDIM)
        level = level_ref[head : head + 1, :]
        base = width + 16 * other
        sent = sent_ref[base : base + 16, :].astype(F32)
        their_level = sent[0:1] + sent[1:2] + sent[2:3]
        top = jnp.maximum(level, their_level)
        my_part = jnp.exp2(level - top)
        their_part = jnp.exp2(their_level - top)
        scale = 1.0 / (my_part + their_part)
        merged = keep_ref[rows, :] * (my_part * scale)
        merged = merged + sent_ref[other_rows, :].astype(F32) * (their_part * scale)
        pieces.append(merged.astype(BF16))
    attended = jnp.concatenate(pieces, axis=0).T
    halfway = width // 2
    projected = dot(attended[:, :halfway], w_out_own[...]) + dot(
        attended[:, halfway:], w_out_other[...]
    )
    resid = (tokens_ref[...].astype(F32) + projected).astype(BF16)
    normed = layer_norm(resid, gain_ref[...], bias_ref[...]).astype(BF16)
    total = resid.astype(F32)
    chunk = 512
    for up, down in ((w_up_own, w_down_own), (w_up_other, w_down_other)):
        for start in range(0, up.shape[1], chunk):
            raised = dot(normed, up[:, start : start + chunk])
            hidden = (raised * (1.0 + lax.erf(raised * (0.5**0.5))) * 0.5).astype(BF16)
            total = total + dot(hidden, down[start : start + chunk, :])
    out_ref[...] = total.astype(BF16)


def tail(place, sent, keep, level, tokens, gain, bias, weights):
    rows, width = tokens.shape
    sent_rows = sent.shape[0] // 2
    vector = pl.BlockSpec((1, width), lambda i, s, c: (0, 0))
    grid_spec = pltpu.PrefetchScalarGridSpec(
        num_scalar_prefetch=2,
        grid=(1,),
        in_specs=[
            pl.BlockSpec((sent_rows, rows), lambda i, s, c: (1 - c[0], 0)),
            pl.BlockSpec(keep.shape, lambda i, s, c: (0, 0)),
            pl.BlockSpec(level.shape, lambda i, s, c: (0, 0)),
            pl.BlockSpec((rows, width), lambda i, s, c: (0, 0)),
            vector,
            vector,
        ]
        + [in_vmem()] * len(weights),
        out_specs=pl.BlockSpec((rows, width), lambda i, s, c: (0, 0)),
    )
    return pl.pallas_call(
        tail_kernel,
        grid_spec=grid_spec,
        out_shape=jax.ShapeDtypeStruct(tokens.shape, BF16),
        compiler_params=params(8),
        name="tail",
    )(
        *place,
        sent,
        keep,
        level,
        tokens,
        gain.reshape(1, -1),
        bias.reshape(1, -1),
        *[held(weight) for weight in weights],
    )


def from_partner(array):
    return lax.ppermute(array, "head", [(0, 1), (1, 0)])


def from_block(array, distance):
    blocks = lax.axis_size("seq")
    ahead = [(2 * i, 2 * (i + distance)) for i in range(blocks - distance)]
    behind = [(2 * i + 1, 2 * (i - distance) + 1) for i in range(distance, blocks)]
    return lax.ppermute(array, ("seq", "head"), ahead + behind)


def shards(tokens, ln1_gain, ln1_bias, w_qkv, w_out, ln2_gain, ln2_bias, w_up, w_down, block_mask):
    here = lax.axis_index("seq")
    core = lax.axis_index("head")
    place = (here.astype(jnp.int32).reshape(1), core.astype(jnp.int32).reshape(1))
    w_own = jnp.transpose(w_qkv, (1, 0, 2))
    mine = norm_rows(place, tokens, ln1_gain, ln1_bias)
    both = lax.all_gather(mine, "head", axis=0, tiled=True)
    near = {}
    for d in range(1, REACH + 1):
        near[d] = from_block(both, d)
    w_other = from_partner(w_own)
    w_out_other = from_partner(w_out)
    w_up_other = from_partner(w_up)
    w_down_other = from_partner(w_down)
    queries, acc, stats, w_kept = own_attention(both, mine, w_own, w_other)
    loads = ((w_out, w_up, w_down), (w_out_other, w_up_other, w_down_other))
    weights = []
    for part, distances in enumerate(BLOCK_ORDER):
        acc, stats, loaded = block_attention(
            place,
            block_mask,
            queries,
            w_kept,
            w_other,
            [(d, near[d]) for d in distances],
            acc,
            stats,
            loads[part],
        )
        weights.append(loaded)
    packed, keep, level = pack(place, acc, stats)
    sent = lax.all_gather(packed, "head", axis=0, tiled=True)
    ordered = [weight for both_halves in zip(*weights) for weight in both_halves]
    return tail(place, sent, keep, level, tokens, ln2_gain, ln2_bias, ordered)


BLOCK_ORDER = ((1, 3), (4, 2))


def solution(mesh):
    in_specs = (
        P(("seq", "head"), None),
        P(),
        P(),
        P(None, None, "head"),
        P("head", None),
        P(),
        P(),
        P(None, "head"),
        P("head", None),
        P(),
    )
    out_specs = P(("seq", "head"), None)
    return jax.shard_map(
        shards, mesh=mesh, in_specs=in_specs, out_specs=out_specs, check_vma=False
    )
```

time: 200 us -> 82.6 us (0.41)
  the two profiles are of different devices: /device:TPU:1 before, /device:TPU:195 now
where the time goes in v2:
time: 82.6 us; the launch traced here: 82.2 us
  Pallas kernels  30.5 us (37%)
  starting transfers between devices  28.9 us (35%)
  blocking collectives  13.8 us (17%)
  waiting for transfers between devices  6.87 us (8%)
  local copies, waits for them, and re-layouts  1.98 us (2%)
    pallas_call x2, Pallas kernels, block_attention(): pl.pallas_call(body, grid_spec=grid_spec, out_shape=[vmem_out(acc.shape,...  18.6 us
    ppermute x4, starting transfers between devices, from_block(): return lax.ppermute(array, ('seq', 'head'), ahead + behind)  16.8 us
    ppermute x4, starting transfers between devices, from_partner(): return lax.ppermute(array, 'head', [(0, 1), (1, 0)])  12.1 us
    all_gather x1, blocking collectives, shards(): both = lax.all_gather(mine, 'head', axis=0, tiled=True)  11.5 us
    ppermute x4, waiting for transfers between devices, from_block(): return lax.ppermute(array, ('seq', 'head'), ahead + behind)  6.86 us
    pallas_call x1, Pallas kernels, own_attention(): pl.pallas_call(own_kernel, in_specs=[in_vmem(), in_vmem(), pl.BlockSpec(m...  4.96 us
    pallas_call x1, Pallas kernels, tail(): pl.pallas_call(tail_kernel, grid_spec=grid_spec, out_shape=jax.ShapeDtype...  4.82 us
    all_gather x1, blocking collectives, shards(): sent = lax.all_gather(packed, 'head', axis=0, tiled=True)  2.28 us
  transfers between devices with their start and end apart: 8, of which 2 were waited for; matrix products, arithmetic and copies ran while one was open for 0% of the time, Pallas kernels for 20%

profile of v2, /device:TPU:195, one launch (start us, length us, event | category | flops | bytes accessed | tf_op | source)
XLA Modules:
  0.0 82.2 jit_solution(128052757626190326)
XLA Ops:
  0.0 2.6 %collective-permute-start.4 = (bf16[1024,2048]{1,0:T(8,128)(2,1)}, bf16[1024,2048]{1,0:T(8,128)(2,1)}, u32[]{:S(2)}, u32[]{:S(2)}) collective-permute-start(bf16[1024,2048]{1,0:T(8,128)(2,1)} %refs_9_.1), channel_id=1, source_target_pairs={{0,1},{1,0},{2,3},{3,2},{4,5},{5,4},{6,7},{7,6},{8,9},{9,8},{10,11... | collective-permute-start | bytes 12582920 | tf_op jit(solution)/shard_map/ppermute | solution.py:383
  2.6 1.9 %collective-permute-start.5 = (bf16[2048,1024]{1,0:T(8,128)(2,1)}, bf16[2048,1024]{1,0:T(8,128)(2,1)}, u32[]{:S(2)}, u32[]{:S(2)}) collective-permute-start(bf16[2048,1024]{1,0:T(8,128)(2,1)} %refs_10_.1), channel_id=1, source_target_pairs={{0,1},{1,0},{2,3},{3,2},{4,5},{5,4},{6,7},{7,6},{8,9},{9,8},{10,11... | collective-permute-start | bytes 12582920 | tf_op jit(solution)/shard_map/ppermute | solution.py:383
  4.5 2.4 %collective-permute-start = (bf16[3,1024,512]{2,1,0:T(8,128)(2,1)}, bf16[3,1024,512]{2,1,0:T(8,128)(2,1)S(1)}, u32[]{:S(2)}, u32[]{:S(2)}) collective-permute-start(bf16[3,1024,512]{2,1,0:T(8,128)(2,1)} %bitcast.9), channel_id=1, source_target_pairs={{0,1},{1,0},{2,3},{3,2},{4,5},{5,4},{6,7},{7,6},{8,9},{9,8},{10,11... | collective-permute-start | bytes 9437192 | tf_op jit(solution)/shard_map/ppermute | solution.py:383
  6.9 0.0 copy-start.1
  6.9 2.0 %norm_rows.1.mine_ref = bf16[128,1024]{1,0:T(8,128)(2,1)} custom-call(s32[1]{0:T(128)} %bitcast.here_ref.refs_0_, s32[1]{0:T(128)} %bitcast.1.core_ref.refs_1_, bf16[128,1024]{1,0:T(8,128)(2,1)} %tokens_ref.3, f32[1,1024]{1,0:T(1,128)} %bitcast.11, f32[1,1024]{1,0:T(1,128)} %bitcast.12), custom_call_target="tpu_custom_call" | custom-call | tf_op jit(solution)/shard_map/norm_rows/pallas_call | solution.py:64
  8.9 11.5 %all_gather.6.both_ref = bf16[256,1024]{1,0:T(8,128)(2,1)S(1)} all-gather(bf16[128,1024]{1,0:T(8,128)(2,1)} %norm_rows.1.mine_ref), channel_id=1, replica_groups=mesh['seq'=256,'head'=2] {'head'}, dimensions={0}, use_global_device_ids=true | all-gather | bytes 786432 | tf_op jit(solution)/shard_map/all_gather | solution.py:399
  20.4 5.1 %collective-permute-start.7 = (bf16[256,1024]{1,0:T(8,128)(2,1)S(1)}, bf16[256,1024]{1,0:T(8,128)(2,1)S(1)}, u32[]{:S(2)}, u32[]{:S(2)}) collective-permute-start(bf16[256,1024]{1,0:T(8,128)(2,1)S(1)} %all_gather.6.both_ref), channel_id=1, source_target_pairs={{0,6},{2,8},{4,10},{6,12},{8,14},{10,16},{12,18},{14,20},{16,22},{... | collective-permute-start | bytes 1572872 | tf_op jit(solution)/shard_map/ppermute | solution.py:390
  25.5 2.2 %collective-permute-start.6 = (bf16[256,1024]{1,0:T(8,128)(2,1)S(1)}, bf16[256,1024]{1,0:T(8,128)(2,1)S(1)}, u32[]{:S(2)}, u32[]{:S(2)}) collective-permute-start(bf16[256,1024]{1,0:T(8,128)(2,1)S(1)} %all_gather.6.both_ref), channel_id=1, source_target_pairs={{0,2},{2,4},{4,6},{6,8},{8,10},{10,12},{12,14},{14,16},{16,18},{18... | collective-permute-start | bytes 1572872 | tf_op jit(solution)/shard_map/ppermute | solution.py:390
  27.7 3.9 %collective-permute-done.7.refs_7_ = bf16[256,1024]{1,0:T(8,128)(2,1)S(1)} collective-permute-done((bf16[256,1024]{1,0:T(8,128)(2,1)S(1)}, bf16[256,1024]{1,0:T(8,128)(2,1)S(1)}, u32[]{:S(2)}, u32[]{:S(2)}) %collective-permute-start.7) | collective-permute-done | bytes 524320 | tf_op jit(solution)/shard_map/ppermute | solution.py:390
  31.6 5.2 %collective-permute-start.3 = (bf16[512,1024]{1,0:T(8,128)(2,1)}, bf16[512,1024]{1,0:T(8,128)(2,1)S(1)}, u32[]{:S(2)}, u32[]{:S(2)}) collective-permute-start(bf16[512,1024]{1,0:T(8,128)(2,1)} %refs_8_.1), channel_id=1, source_target_pairs={{0,1},{1,0},{2,3},{3,2},{4,5},{5,4},{6,7},{7,6},{8,9},{9,8},{10,11... | collective-permute-start | bytes 3145736 | tf_op jit(solution)/shard_map/ppermute | solution.py:383
  36.9 2.9 %collective-permute-done.6.refs_6_ = bf16[256,1024]{1,0:T(8,128)(2,1)S(1)} collective-permute-done((bf16[256,1024]{1,0:T(8,128)(2,1)S(1)}, bf16[256,1024]{1,0:T(8,128)(2,1)S(1)}, u32[]{:S(2)}, u32[]{:S(2)}) %collective-permute-start.6) | collective-permute-done | bytes 524320 | tf_op jit(solution)/shard_map/ppermute | solution.py:390
  39.8 4.9 %collective-permute-start.2 = (bf16[256,1024]{1,0:T(8,128)(2,1)S(1)}, bf16[256,1024]{1,0:T(8,128)(2,1)S(1)}, u32[]{:S(2)}, u32[]{:S(2)}) collective-permute-start(bf16[256,1024]{1,0:T(8,128)(2,1)S(1)} %all_gather.6.both_ref), channel_id=1, source_target_pairs={{0,4},{2,6},{4,8},{6,10},{8,12},{10,14},{12,16},{14,18},{16,20},{1... | collective-permute-start | bytes 1572872 | tf_op jit(solution)/shard_map/ppermute | solution.py:390
  44.7 0.0 collective-permute-done.w_other_ref.refs_5_
  44.7 4.6 %collective-permute-start.1 = (bf16[256,1024]{1,0:T(8,128)(2,1)S(1)}, bf16[256,1024]{1,0:T(8,128)(2,1)S(1)}, u32[]{:S(2)}, u32[]{:S(2)}) collective-permute-start(bf16[256,1024]{1,0:T(8,128)(2,1)S(1)} %all_gather.6.both_ref), channel_id=1, source_target_pairs={{0,8},{2,10},{4,12},{6,14},{8,16},{10,18},{12,20},{14,22},{16,24},... | collective-permute-start | bytes 1572872 | tf_op jit(solution)/shard_map/ppermute | solution.py:390
  49.4 0.0 copy-start
  49.4 0.9 %copy-done = bf16[128,1024]{1,0:T(8,128)(2,1)S(1)} copy-done((bf16[128,1024]{1,0:T(8,128)(2,1)S(1)}, bf16[128,1024]{1,0:T(8,128)(2,1)}, u32[]{:S(2)}) %copy-start) | copy-done | bytes 262168
  50.3 5.0 %own_attention.1 = (bf16[8,128,512]{2,1,0:T(8,128)(2,1)S(1)}, f32[1024,256]{1,0:T(8,128)S(1)}, f32[8,8,512]{2,1,0:T(8,128)S(1)}, bf16[3,1024,512]{2,1,0:T(8,128)(2,1)S(1)}) custom-call(bf16[256,1024]{1,0:T(8,128)(2,1)S(1)} %all_gather.6.both_ref, bf16[128,1024]{1,0:T(8,128)(2,1)S(1)} %copy-done, bf16[3,1024,512]{2,1,0:T(8,128)(2,1)} %bitcast.10, ...), custom_call_target="tpu_custom_call" | custom-call | tf_op jit(solution)/shard_map/own_attention/pallas_call | solution.py:146
  55.3 0.0 copy-done.1
  55.3 9.2 %block_attention.2 = (f32[1024,256]{1,0:T(8,128)S(1)}, f32[8,8,512]{2,1,0:T(8,128)S(1)}, bf16[512,1024]{1,0:T(8,128)(2,1)S(1)}, bf16[1024,2048]{1,0:T(8,128)(2,1)S(1)}, bf16[2048,1024]{1,0:T(8,128)(2,1)S(1)}) custom-call(s32[1]{0:T(128)} %bitcast.here_ref.refs_0_, s32[1]{0:T(128)} %bitcast.1.core_ref.refs_1_, ...), custom_call_target="tpu_custom_call", output_to_operand_aliasing={{0}: (11, {}), {1}: (12, {})} | custom-call | tf_op jit(solution)/shard_map/block_attention/pallas_call | solution.py:215
  64.5 0.0 collective-permute-done.2.refs_7_
  64.5 0.0 collective-permute-done.1.refs_6_
  64.5 0.0 collective-permute-done.3.refs_8_
  64.5 0.0 copy-start.5
  64.5 0.0 collective-permute-done.4.refs_9_
  64.6 0.0 collective-permute-done.5.refs_10_
  64.6 1.0 %copy-done.5 = bf16[512,1024]{1,0:T(8,128)(2,1)} copy-done((bf16[512,1024]{1,0:T(8,128)(2,1)}, bf16[512,1024]{1,0:T(8,128)(2,1)S(1)}, u32[]{:S(2)}) %copy-start.5) | copy-done | bytes 1048600
  65.6 0.0 copy-start.2
  65.6 0.0 copy-start.3
  65.6 0.0 copy-start.4
  65.6 9.4 %block_attention.3 = (f32[1024,256]{1,0:T(8,128)S(1)}, f32[8,8,512]{2,1,0:T(8,128)S(1)}, bf16[512,1024]{1,0:T(8,128)(2,1)S(1)}, bf16[1024,2048]{1,0:T(8,128)(2,1)S(1)}, bf16[2048,1024]{1,0:T(8,128)(2,1)S(1)}) custom-call(s32[1]{0:T(128)} %bitcast.here_ref.refs_0_, s32[1]{0:T(128)} %bitcast.1.core_ref.refs_1_, ...), custom_call_target="tpu_custom_call", output_to_operand_aliasing={{0}: (11, {}), {1}: (12, {})} | custom-call | tf_op jit(solution)/shard_map/block_attention/pallas_call | solution.py:215
  75.0 0.1 pack.1
  75.1 2.3 %all_gather.7.sent_ref = bf16[2560,128]{1,0:T(8,128)(2,1)S(1)} all-gather(bf16[1280,128]{1,0:T(8,128)(2,1)S(1)} %get-tuple-element.30), channel_id=1, replica_groups=mesh['seq'=256,'head'=2] {'head'}, dimensions={0}, use_global_device_ids=true | all-gather | bytes 983040 | tf_op jit(solution)/shard_map/all_gather | solution.py:424
  77.4 0.0 copy-done.2
  77.4 0.0 copy-done.3
  77.4 0.0 copy-done.4
  77.4 4.8 %tail.1 = bf16[128,1024]{1,0:T(8,128)(2,1)} custom-call(s32[1]{0:T(128)} %bitcast.here_ref.refs_0_, s32[1]{0:T(128)} %bitcast.1.core_ref.refs_1_, bf16[2560,128]{1,0:T(8,128)(2,1)S(1)} %all_gather.7.sent_ref, f32[1024,128]{1,0:T(8,128)S(1)} %get-tuple-element.31.keep_ref, f32[16,128]{1,0:T(8,128)S(1)} %get-tuple-element.32.level_ref, ...), custom_call_target="tpu_custom_call" | custom-call | tf_op jit(solution)/shard_map/tail/pallas_call | solution.py:364
Async XLA Ops:
  0.0 64.6 %collective-permute-start.4 = (bf16[1024,2048]{1,0:T(8,128)(2,1)}, bf16[1024,2048]{1,0:T(8,128)(2,1)}, u32[]{:S(2)}, u32[]{:S(2)}) collective-permute-start(bf16[1024,2048]{1,0:T(8,128)(2,1)} %refs_9_.1), channel_id=1, source_target_pairs={{0,1},{1,0},{2,3},{3,2},{4,5},{5,4},{6,7},{7,6},{8,9},{9,8},{10,11... | collective-permute-start | bytes 12582920 | tf_op jit(solution)/shard_map/ppermute | solution.py:383
  2.6 62.0 %collective-permute-start.5 = (bf16[2048,1024]{1,0:T(8,128)(2,1)}, bf16[2048,1024]{1,0:T(8,128)(2,1)}, u32[]{:S(2)}, u32[]{:S(2)}) collective-permute-start(bf16[2048,1024]{1,0:T(8,128)(2,1)} %refs_10_.1), channel_id=1, source_target_pairs={{0,1},{1,0},{2,3},{3,2},{4,5},{5,4},{6,7},{7,6},{8,9},{9,8},{10,11... | collective-permute-start | bytes 12582920 | tf_op jit(solution)/shard_map/ppermute | solution.py:383
  4.5 40.2 %collective-permute-start = (bf16[3,1024,512]{2,1,0:T(8,128)(2,1)}, bf16[3,1024,512]{2,1,0:T(8,128)(2,1)S(1)}, u32[]{:S(2)}, u32[]{:S(2)}) collective-permute-start(bf16[3,1024,512]{2,1,0:T(8,128)(2,1)} %bitcast.9), channel_id=1, source_target_pairs={{0,1},{1,0},{2,3},{3,2},{4,5},{5,4},{6,7},{7,6},{8,9},{9,8},{10,11... | collective-permute-start | bytes 9437192 | tf_op jit(solution)/shard_map/ppermute | solution.py:383
  6.9 48.4 %copy-start.1 = (s32[256,256]{1,0:T(8,128)S(1)}, s32[256,256]{1,0:T(8,128)}, u32[]{:S(2)}) copy-start(s32[256,256]{1,0:T(8,128)} %refs_2_.3) | copy-start | bytes 786436
  20.4 11.2 %collective-permute-start.7 = (bf16[256,1024]{1,0:T(8,128)(2,1)S(1)}, bf16[256,1024]{1,0:T(8,128)(2,1)S(1)}, u32[]{:S(2)}, u32[]{:S(2)}) collective-permute-start(bf16[256,1024]{1,0:T(8,128)(2,1)S(1)} %all_gather.6.both_ref), channel_id=1, source_target_pairs={{0,6},{2,8},{4,10},{6,12},{8,14},{10,16},{12,18},{14,20},{16,22},{... | collective-permute-start | bytes 1572872 | tf_op jit(solution)/shard_map/ppermute | solution.py:390
  25.5 14.3 %collective-permute-start.6 = (bf16[256,1024]{1,0:T(8,128)(2,1)S(1)}, bf16[256,1024]{1,0:T(8,128)(2,1)S(1)}, u32[]{:S(2)}, u32[]{:S(2)}) collective-permute-start(bf16[256,1024]{1,0:T(8,128)(2,1)S(1)} %all_gather.6.both_ref), channel_id=1, source_target_pairs={{0,2},{2,4},{4,6},{6,8},{8,10},{10,12},{12,14},{14,16},{16,18},{18... | collective-permute-start | bytes 1572872 | tf_op jit(solution)/shard_map/ppermute | solution.py:390
  31.6 32.9 %collective-permute-start.3 = (bf16[512,1024]{1,0:T(8,128)(2,1)}, bf16[512,1024]{1,0:T(8,128)(2,1)S(1)}, u32[]{:S(2)}, u32[]{:S(2)}) collective-permute-start(bf16[512,1024]{1,0:T(8,128)(2,1)} %refs_8_.1), channel_id=1, source_target_pairs={{0,1},{1,0},{2,3},{3,2},{4,5},{5,4},{6,7},{7,6},{8,9},{9,8},{10,11... | collective-permute-start | bytes 3145736 | tf_op jit(solution)/shard_map/ppermute | solution.py:383
  39.8 24.7 %collective-permute-start.2 = (bf16[256,1024]{1,0:T(8,128)(2,1)S(1)}, bf16[256,1024]{1,0:T(8,128)(2,1)S(1)}, u32[]{:S(2)}, u32[]{:S(2)}) collective-permute-start(bf16[256,1024]{1,0:T(8,128)(2,1)S(1)} %all_gather.6.both_ref), channel_id=1, source_target_pairs={{0,4},{2,6},{4,8},{6,10},{8,12},{10,14},{12,16},{14,18},{16,20},{1... | collective-permute-start | bytes 1572872 | tf_op jit(solution)/shard_map/ppermute | solution.py:390
  44.7 19.8 %collective-permute-start.1 = (bf16[256,1024]{1,0:T(8,128)(2,1)S(1)}, bf16[256,1024]{1,0:T(8,128)(2,1)S(1)}, u32[]{:S(2)}, u32[]{:S(2)}) collective-permute-start(bf16[256,1024]{1,0:T(8,128)(2,1)S(1)} %all_gather.6.both_ref), channel_id=1, source_target_pairs={{0,8},{2,10},{4,12},{6,14},{8,16},{10,18},{12,20},{14,22},{16,24},... | collective-permute-start | bytes 1572872 | tf_op jit(solution)/shard_map/ppermute | solution.py:390
  49.4 1.0 %copy-start = (bf16[128,1024]{1,0:T(8,128)(2,1)S(1)}, bf16[128,1024]{1,0:T(8,128)(2,1)}, u32[]{:S(2)}) copy-start(bf16[128,1024]{1,0:T(8,128)(2,1)} %norm_rows.1.mine_ref) | copy-start | bytes 786436
  64.5 1.1 %copy-start.5 = (bf16[512,1024]{1,0:T(8,128)(2,1)}, bf16[512,1024]{1,0:T(8,128)(2,1)S(1)}, u32[]{:S(2)}) copy-start(bf16[512,1024]{1,0:T(8,128)(2,1)S(1)} %collective-permute-done.3.refs_8_) | copy-start | bytes 3145732
  65.6 11.8 %copy-start.2 = (bf16[128,1024]{1,0:T(8,128)(2,1)S(1)}, bf16[128,1024]{1,0:T(8,128)(2,1)}, u32[]{:S(2)}) copy-start(bf16[128,1024]{1,0:T(8,128)(2,1)} %tokens_ref.3) | copy-start | bytes 786436
  65.6 11.8 %copy-start.3 = (f32[1024]{0:T(1024)S(1)}, f32[1024]{0:T(1024)}, u32[]{:S(2)}) copy-start(f32[1024]{0:T(1024)} %param.15) | copy-start | bytes 12292
  65.6 11.8 %copy-start.4 = (f32[1024]{0:T(1024)S(1)}, f32[1024]{0:T(1024)}, u32[]{:S(2)}) copy-start(f32[1024]{0:T(1024)} %param.16) | copy-start | bytes 12292
